TPU v7x, 32 devices: a whole 2x2x4 slice. The times are simulated.
32 devices in a mesh: expert: 16 (over z, y, x), tok: 2 (over core).
Axes of the slice: x: 2, y: 2, z: 4, core: 2. Of those that a mesh axis runs over, the one named last changes fastest.
Arguments:
- tokens: bfloat16 [2048, 3584], P(('expert', 'tok')), may hold values from -6 to 6
- routes: int32 [2048, 8], P(('expert', 'tok')), may hold values from 0 to 15, all different within a row; in each aligned block of 64 rows (0 to 63, 64 to 127, ...) at most 36 rows name the same one
- gates: float32 [2048, 8], P(('expert', 'tok')), may hold values from 0.05 to 1
- upstream: bfloat16 [2048, 3584], P(('expert', 'tok')), may hold values from -6 to 6
- w_up: bfloat16 [16, 3584, 1024], P('expert', None, 'tok'), may hold values from -0.09375 to 0.09375
- w_down: bfloat16 [16, 1024, 3584], P('expert', 'tok'), may hold values from -0.1875 to 0.1875
Outputs:
- mixed: bfloat16 [2048, 3584], P(('expert', 'tok'))
- d_tokens: bfloat16 [2048, 3584], P(('expert', 'tok'))
- d_gates: float32 [2048, 8], P(('expert', 'tok'))
- grad_up: bfloat16 [16, 3584, 1024], P('expert', None, 'tok')
- grad_down: bfloat16 [16, 1024, 3584], P('expert', 'tok')
Inputs may be any that keep to these rules, and one draw needn't show every extreme that they name: `routes`: each token names 8 different experts. At most 36 of the 64 tokens of one device name the same expert, and in every draw the tokens of some device name some expert exactly 36 times.
All inputs are finite; a program needn't handle non-finite values.
Results may differ from a plain program's by a relative error of at most 0.0065.
Values may be sent and summed in bfloat16 or wider, within the bound.
A program may use at most 192 MiB of HBM per device.

v0:
```python
import jax
import jax.numpy as jnp
from jax import lax
from jax.sharding import PartitionSpec as P

GELU_C = 0.7978845608028654
GELU_A = 0.044715


def gelu_value(hidden):
    inner_arg = GELU_C * (hidden + GELU_A * hidden * hidden * hidden)
    return 0.5 * hidden * (1.0 + jnp.tanh(inner_arg))


def gelu_slope(hidden):
    tangent = jnp.tanh(GELU_C * (hidden + GELU_A * hidden * hidden * hidden))
    return 0.5 * (1.0 + tangent) + 0.5 * hidden * (1.0 - tangent * tangent) * GELU_C * (
        1.0 + 3.0 * GELU_A * hidden * hidden
    )


def expert_rows(rows_x, rows_grad, up_local, down_local):
    hidden = jnp.dot(rows_x, up_local, preferred_element_type=jnp.float32)
    active = gelu_value(hidden).astype(jnp.bfloat16)
    out_part = jnp.dot(active, down_local, preferred_element_type=jnp.float32)
    d_active = lax.dot_general(
        rows_grad, down_local, (((1,), (1,)), ((), ())), preferred_element_type=jnp.float32
    )
    d_hidden = (d_active * gelu_slope(hidden)).astype(jnp.bfloat16)
    dx_part = lax.dot_general(
        d_hidden, up_local, (((1,), (1,)), ((), ())), preferred_element_type=jnp.float32
    )
    grad_down = lax.dot_general(
        active, rows_grad, (((0,), (0,)), ((), ())), preferred_element_type=jnp.float32
    )
    grad_up = lax.dot_general(
        rows_x, d_hidden, (((0,), (0,)), ((), ())), preferred_element_type=jnp.float32
    )
    return (out_part, dx_part, grad_up, grad_down)


def routed_shards(tokens, routes, gates, upstream, w_up, w_down):
    tok_rows, feature_width = tokens.shape
    top_count = routes.shape[1]
    owners = lax.axis_size("expert")
    pair_count = lax.axis_size("tok")
    capacity = tok_rows * top_count // owners + max(1, tok_rows * top_count // (8 * owners))
    assigned = routes.reshape(-1)
    labels = jnp.arange(owners, dtype=jnp.int32)
    onehot = (assigned[:, None] == labels[None, :]).astype(jnp.int32)
    earlier = jnp.cumsum(onehot, axis=0) - onehot
    slot_rank = jnp.sum(earlier * onehot, axis=1)
    slot_of = assigned * capacity + slot_rank
    slot_ids = jnp.arange(owners * capacity, dtype=jnp.int32)
    matches = (slot_of[None, :] == slot_ids[:, None]).astype(jnp.int32)
    filled = jnp.sum(matches, axis=1) > 0
    source = jnp.sum(matches * jnp.arange(assigned.shape[0], dtype=jnp.int32)[None, :], axis=1)
    token_ids = source // top_count
    send_x = jnp.where(filled[:, None], tokens[token_ids], jnp.zeros((), jnp.bfloat16))
    gate_rows = jnp.where(filled, gates.reshape(-1)[source], jnp.zeros((), jnp.float32))
    send_grad = (gate_rows[:, None] * upstream[token_ids].astype(jnp.float32)).astype(jnp.bfloat16)
    send_x = send_x.reshape(owners, capacity, feature_width)
    send_grad = send_grad.reshape(owners, capacity, feature_width)
    recv_x, recv_grad = (
        lax.all_to_all(send_x, "expert", split_axis=0, concat_axis=0, tiled=True),
        lax.all_to_all(send_grad, "expert", split_axis=0, concat_axis=0, tiled=True),
    )
    both_x, both_grad = (
        lax.all_gather(recv_x[None], "tok", axis=0, tiled=True),
        lax.all_gather(recv_grad[None], "tok", axis=0, tiled=True),
    )
    rows_x = both_x.reshape(-1, feature_width)
    rows_grad = both_grad.reshape(-1, feature_width)
    out_part, dx_part, grad_up, grad_down = expert_rows(rows_x, rows_grad, w_up[0], w_down[0])
    shaped_out = out_part.reshape(pair_count, owners, capacity, feature_width)
    shaped_dx = dx_part.reshape(pair_count, owners, capacity, feature_width)
    summed_out, summed_dx = (
        lax.psum_scatter(shaped_out, "tok", scatter_dimension=0, tiled=True),
        lax.psum_scatter(shaped_dx, "tok", scatter_dimension=0, tiled=True),
    )
    home_out, home_dx = (
        lax.all_to_all(
            summed_out[0].astype(jnp.bfloat16), "expert", split_axis=0, concat_axis=0, tiled=True
        ),
        lax.all_to_all(
            summed_dx[0].astype(jnp.bfloat16), "expert", split_axis=0, concat_axis=0, tiled=True
        ),
    )
    out_pairs = (
        home_out.reshape(owners * capacity, feature_width)[slot_of]
        .reshape(tok_rows, top_count, feature_width)
        .astype(jnp.float32)
    )
    dx_pairs = (
        home_dx.reshape(owners * capacity, feature_width)[slot_of]
        .reshape(tok_rows, top_count, feature_width)
        .astype(jnp.float32)
    )
    mixed_out = jnp.sum(gates[:, :, None] * out_pairs, axis=1).astype(jnp.bfloat16)
    d_gates = jnp.sum(upstream.astype(jnp.float32)[:, None, :] * out_pairs, axis=2)
    d_tokens = jnp.sum(dx_pairs, axis=1).astype(jnp.bfloat16)
    return (
        mixed_out,
        d_tokens,
        d_gates,
        grad_up.astype(jnp.bfloat16)[None],
        grad_down.astype(jnp.bfloat16)[None],
    )


def swapped(array, bit):
    return lax.ppermute(array, "expert", tuple(((i, i ^ bit) for i in range(16))))


def shifted(array, step, senders):
    return lax.ppermute(
        array,
        "expert",
        tuple(((i, i + 4 * step) for z in senders for i in range(4 * z, 4 * z + 4))),
    )


def add_rows(first, *others):
    total = first.astype(jnp.float32)
    for other in others:
        total = total + other.astype(jnp.float32)
    return total.astype(jnp.bfloat16)


def gathered_slots(block, layer, first, second):
    up_one = shifted(block, 1, (0, 1, 2))
    down_one = shifted(block, -1, (3, 2, 1))
    up_two = shifted(up_one, 1, (1, 2))
    down_two = shifted(down_one, -1, (2, 1))
    up_three = shifted(up_two, 1, (2,))
    down_three = shifted(down_two, -1, (1,))
    low = layer < 2
    far = jnp.where(
        low, jnp.where(layer == 0, down_three, up_one), jnp.where(layer == 3, up_three, down_one)
    )
    columns = (block, jnp.where(low, down_one, up_one), jnp.where(low, down_two, up_two), far)
    slots = []
    for column in columns:
        pair = jnp.stack([column, swapped(column, first)])
        other = swapped(pair, second)
        if first == 1:
            slots.append(jnp.concatenate([pair[0], pair[1], other[0], other[1]], axis=0))
        else:
            slots.append(jnp.concatenate([pair[0], other[0], pair[1], other[1]], axis=0))
    return slots


def scattered_column(rows, tok_rows, first, second):
    blocks = [rows[i * tok_rows : (i + 1) * tok_rows].astype(jnp.bfloat16) for i in range(4)]
    kept, sent = ((0, 1), (2, 3)) if first == 2 else ((0, 2), (1, 3))
    came = swapped(jnp.stack([blocks[i] for i in sent]), first)
    near = add_rows(blocks[kept[0]], came[0])
    far = add_rows(blocks[kept[1]], came[1])
    return add_rows(near, swapped(far, second))


def scattered_layers(columns, layer):
    up = shifted(columns[3], 1, (0,))
    down = shifted(columns[3], -1, (3,))
    up = shifted(add_rows(columns[2], up), 1, (0, 1))
    down = shifted(add_rows(columns[2], down), -1, (3, 2))
    up = shifted(add_rows(jnp.where(layer == 2, columns[3], columns[1]), up), 1, (0, 1, 2))
    down = shifted(add_rows(jnp.where(layer == 1, columns[3], columns[1]), down), -1, (3, 2, 1))
    return add_rows(columns[0], up, down)


def transposed_dot(rows, weights):
    return lax.dot_general(
        rows, weights, (((1,), (1,)), ((), ())), preferred_element_type=jnp.float32
    )


def outer(rows, columns):
    return lax.dot_general(
        rows, columns, (((0,), (0,)), ((), ())), preferred_element_type=jnp.float32
    )


def dense_shards(tokens, routes, gates, upstream, w_up, w_down):
    tok_rows, width = tokens.shape
    owners = lax.axis_size("expert")
    half = w_up.shape[2]
    swap = ((0, 1), (1, 0))
    mine = lax.axis_index("expert")
    layer = mine // 4
    up_local, down_local = (w_up[0], w_down[0])
    named = routes[:, :, None] == jnp.arange(owners, dtype=jnp.int32)
    gate_of = jnp.sum(jnp.where(named, gates[:, :, None], 0.0), axis=1)
    gate_all = lax.all_gather(gate_of, "expert", axis=0, tiled=True).reshape(
        owners, tok_rows, owners
    )
    gate_mine = lax.dynamic_index_in_dim(gate_all, mine, axis=2, keepdims=False)
    layers = (
        layer,
        jnp.where(layer < 2, layer + 1, layer - 1),
        jnp.where(layer < 2, layer + 2, layer - 2),
        jnp.where(layer % 2 == 0, 3, 0),
    )
    sources = [jnp.stack([z * 4 + (mine % 4 ^ flip) for flip in range(4)]) for z in layers]
    slots_x = gathered_slots(tokens, layer, 1, 2)
    slots_u = gathered_slots(upstream, layer, 2, 1)
    up_full = jnp.concatenate([up_local, lax.ppermute(up_local, "tok", swap)], axis=1)
    down_full = jnp.concatenate([down_local, lax.ppermute(down_local, "tok", swap)], axis=0)
    gated, slopes, inners = ([None] * 4, [None] * 4, [None] * 4)
    mixed_columns, dx_columns = ([None] * 4, [None] * 4)
    for s in range(4):
        gate = gate_mine[sources[s]].reshape(-1)[:, None]
        hidden = jnp.dot(slots_x[s], up_full, preferred_element_type=jnp.float32)
        value = gelu_value(hidden)
        gated[s] = (gate * value).astype(jnp.bfloat16)
        back = transposed_dot(slots_u[s], down_full)
        inners[s] = jnp.sum(value * back, axis=1).reshape(4, tok_rows)
        slopes[s] = (gate * back * gelu_slope(hidden)).astype(jnp.bfloat16)
    for s in (3, 2, 1, 0):
        out_part = jnp.dot(gated[s], down_full, preferred_element_type=jnp.float32)
        mixed_columns[s] = scattered_column(out_part, tok_rows, 2, 1)
        dx_part = transposed_dot(slopes[s], up_full)
        dx_columns[s] = scattered_column(dx_part, tok_rows, 1, 2)
    mixed = scattered_layers(mixed_columns, layer)
    d_tokens = scattered_layers(dx_columns, layer)
    order = jnp.concatenate(sources)
    inner = jnp.zeros((owners, tok_rows), jnp.float32).at[order].set(jnp.concatenate(inners))
    inner_all = lax.all_gather(inner, "expert", axis=0, tiled=True).reshape(
        owners, owners, tok_rows
    )
    home = lax.dynamic_index_in_dim(inner_all, mine, axis=1, keepdims=False)
    d_gates = jnp.sum(jnp.where(named, home.T[:, None, :], 0.0), axis=2)
    all_x, all_u = (jnp.concatenate(slots_x), jnp.concatenate(slots_u))
    act, d_hidden = (jnp.concatenate(gated), jnp.concatenate(slopes))
    down_far = outer(act[:, half:], all_u).astype(jnp.bfloat16)
    up_far = outer(all_x, d_hidden[:, half:]).astype(jnp.bfloat16)
    down_near = outer(act[:, :half], all_u)
    up_near = outer(all_x, d_hidden[:, :half])
    grad_down = down_near + lax.ppermute(down_far, "tok", swap).astype(jnp.float32)
    grad_up = up_near + lax.ppermute(up_far, "tok", swap).astype(jnp.float32)
    return (
        mixed,
        d_tokens,
        d_gates,
        grad_up.astype(jnp.bfloat16)[None],
        grad_down.astype(jnp.bfloat16)[None],
    )


def shards(tokens, routes, gates, upstream, w_up, w_down):
    dense = lax.axis_size("expert") == 16 and lax.axis_size("tok") == 2
    body = dense_shards if dense else routed_shards
    return body(tokens, routes, gates, upstream, w_up, w_down)


def solution(mesh):
    return jax.shard_map(
        shards,
        mesh=mesh,
        in_specs=(
            P(("expert", "tok"), None),
            P(("expert", "tok"), None),
            P(("expert", "tok"), None),
            P(("expert", "tok"), None),
            P("expert", None, "tok"),
            P("expert", "tok", None),
        ),
        out_specs=(
            P(("expert", "tok"), None),
            P(("expert", "tok"), None),
            P(("expert", "tok"), None),
            P("expert", None, "tok"),
            P("expert", "tok", None),
        ),
        check_vma=False,
    )
```

profile of v0, /device:TPU:20, one launch (start us, length us, event | category | flops | bytes accessed | tf_op | source)
XLA Modules:
  0.0 542.9 jit_solution(3025906620837556485)
XLA Ops:
  0.6 2.5 collective-permute-start.6
  4.7 3.5 collective-permute-start.9
  8.2 2.3 collective-permute-start.34
  18.8 5.5 %collective-permute-done.30 = bf16[64,3584]{1,0:T(8,128)(2,1)S(1)} collective-permute-done((bf16[64,3584]{1,0:T(8,128)(2,1)}, bf16[64,3584]{1,0:T(8,128)(2,1)S(1)}, u32[]{:S(2)}, u32[]{:S(2)}) %collective-permute-start.30) | collective-permute-done | bytes 458784 | tf_op jit(solution)/shard_map/ppermute | solution.py:112
  24.3 3.5 collective-permute-start.37
  27.9 13.7 %collective-permute-done.1 = bf16[2,64,3584]{2,1,0:T(8,128)(2,1)S(1)} collective-permute-done((bf16[2,64,3584]{2,1,0:T(8,128)(2,1)S(1)}, bf16[2,64,3584]{2,1,0:T(8,128)(2,1)S(1)}, u32[]{:S(2)}, u32[]{:S(2)}) %collective-permute-start.1) | collective-permute-done | bytes 917536 | tf_op jit(solution)/shard_map/ppermute | solution.py:112
  43.8 17.9 %collective-permute-done.31 = bf16[2,64,3584]{2,1,0:T(8,128)(2,1)S(1)} collective-permute-done((bf16[2,64,3584]{2,1,0:T(8,128)(2,1)S(1)}, bf16[2,64,3584]{2,1,0:T(8,128)(2,1)S(1)}, u32[]{:S(2)}, u32[]{:S(2)}) %collective-permute-start.31) | collective-permute-done | bytes 917536 | tf_op jit(solution)/shard_map/ppermute | solution.py:112
  63.9 3.2 collective-permute-start.7
  71.0 9.9 %collective-permute-done.16 = bf16[64,3584]{1,0:T(8,128)(2,1)S(1)} collective-permute-done((bf16[64,3584]{1,0:T(8,128)(2,1)S(1)}, bf16[64,3584]{1,0:T(8,128)(2,1)S(1)}, u32[]{:S(2)}, u32[]{:S(2)}) %collective-permute-start.16) | collective-permute-done | bytes 458784 | tf_op jit(solution)/shard_map/ppermute | solution.py:112
  82.4 2.1 collective-permute-start.10
  84.6 17.6 %collective-permute-done.17 = bf16[2,64,3584]{2,1,0:T(8,128)(2,1)S(1)} collective-permute-done((bf16[2,64,3584]{2,1,0:T(8,128)(2,1)S(1)}, bf16[2,64,3584]{2,1,0:T(8,128)(2,1)S(1)}, u32[]{:S(2)}, u32[]{:S(2)}) %collective-permute-start.17) | collective-permute-done | bytes 917536 | tf_op jit(solution)/shard_map/ppermute | solution.py:112
  104.9 17.5 %collective-permute-done.45 = bf16[2,64,3584]{2,1,0:T(8,128)(2,1)S(1)} collective-permute-done((bf16[2,64,3584]{2,1,0:T(8,128)(2,1)S(1)}, bf16[2,64,3584]{2,1,0:T(8,128)(2,1)S(1)}, u32[]{:S(2)}, u32[]{:S(2)}) %collective-permute-start.45) | collective-permute-done | bytes 917536 | tf_op jit(solution)/shard_map/ppermute | solution.py:112
  122.4 2.8 collective-permute-start.35
  133.1 2.1 collective-permute-start.11
  135.2 4.6 collective-permute-done.38
  143.7 4.6 collective-permute-done.20
  150.6 6.1 %collective-permute-done.48 = bf16[64,3584]{1,0:T(8,128)(2,1)S(1)} collective-permute-done((bf16[64,3584]{1,0:T(8,128)(2,1)S(1)}, bf16[64,3584]{1,0:T(8,128)(2,1)S(1)}, u32[]{:S(2)}, u32[]{:S(2)}) %collective-permute-start.48) | collective-permute-done | bytes 458784 | tf_op jit(solution)/shard_map/ppermute | solution.py:112
  159.2 5.4 collective-permute-start.39
  164.6 2.1 fusion.2
  167.3 3.2 multiply_reduce_fusion.3
  170.4 3.0 fusion.18
  173.6 6.8 %multiply_reduce_fusion.2 = (f32[256]{0:T(256)S(1)}, f32[256,1024]{1,0:T(8,128)}) fusion(f32[256,1024]{1,0:T(8,128)} %fusion.18, bf16[512,3584]{1,0:T(8,128)(2,1)} %copy-done.39, bf16[512,3584]{1,0:T(8,128)(2,1)} %bitcast.290, bf16[64,3584]{1,0:T(8,128)(2,1)} %get-tuple-element.58, bf16[64,3584]{1,0:T(8,128)(2,1)S(1)} %collective-permute-done.44, ...), kind=kOutput, calls=%fused_computation.133 | convolution fusion | flops 1903689472 | bytes 11273216 | tf_op jit(solution)/shard_map/dot_general | solution.py:173
  183.1 2.4 constant_dynamic-update-slice_fusion.3
  186.5 11.9 %collective-permute-done.49 = bf16[2,64,3584]{2,1,0:T(8,128)(2,1)S(1)} collective-permute-done((bf16[2,64,3584]{2,1,0:T(8,128)(2,1)}, bf16[2,64,3584]{2,1,0:T(8,128)(2,1)S(1)}, u32[]{:S(2)}, u32[]{:S(2)}) %collective-permute-start.49) | collective-permute-done | bytes 917536 | tf_op jit(solution)/shard_map/ppermute | solution.py:112
  201.0 2.1 fusion.26
  205.0 3.2 multiply_reduce_fusion.1
  211.7 5.0 collective-permute-done.40
  220.1 6.6 %collective-permute-done.13 = bf16[2,64,3584]{2,1,0:T(8,128)(2,1)S(1)} collective-permute-done((bf16[2,64,3584]{2,1,0:T(8,128)(2,1)S(1)}, bf16[2,64,3584]{2,1,0:T(8,128)(2,1)S(1)}, u32[]{:S(2)}, u32[]{:S(2)}) %collective-permute-start.13) | collective-permute-done | bytes 917536 | tf_op jit(solution)/shard_map/ppermute | solution.py:112
  226.8 3.9 collective-permute-done.41
  230.8 3.2 fusion.10
  234.1 3.6 multiply_reduce_fusion
  238.4 33.8 %all_gather.7 = f32[256,64]{1,0:T(8,128)S(1)} all-gather(f32[16,64]{1,0:T(8,128)S(1)} %scatter_custom_fusion), channel_id=1, replica_groups=mesh['expert'=16,'tok'=2] {'expert'}, dimensions={0}, use_global_device_ids=true | all-gather | bytes 69632 | tf_op jit(solution)/shard_map/all_gather | solution.py:228
  272.8 33.2 %all-gather = f32[16,64,16]{1,2,0:T(8,128)S(1)} all-gather(f32[1,64,16]{1,2,0:T(8,128)S(1)} %bitcast.279), channel_id=1, replica_groups=mesh['expert'=16,'tok'=2] {'expert'}, dimensions={0}, use_global_device_ids=true | all-gather | bytes 69632 | tf_op jit(solution)/shard_map/all_gather | solution.py:194
  308.6 2.4 fusion.78
  310.9 5.3 convolution_convert_fusion.5
  316.4 2.5 collective-permute-start.32
  319.8 4.2 convolution_convert_fusion.3
  328.6 5.3 convolution_convert_fusion.4
  334.0 5.3 convolution_convert_fusion.2
  341.7 4.3 convolution_convert_fusion.9
  346.2 4.1 convolution_convert_fusion.7
  350.6 5.2 convolution_convert_fusion.8
  355.9 5.2 convolution_convert_fusion.6
  364.1 8.6 %convolution_convert_fusion = bf16[512,3584]{1,0:T(8,128)(2,1)} fusion(bf16[1024,3584]{1,0:T(8,128)(2,1)} %constant_dynamic-update-slice_fusion.16, bf16[1024,1024]{1,0:T(8,128)(2,1)S(1)} %pad_maximum_fusion.3), kind=kOutput, calls=%fused_computation.9 | convolution fusion | flops 3759931392 | bytes 12058624 | tf_op jit(solution)/shard_map/dot_general | solution.py:179
  374.2 8.6 %convolution_convert_fusion.1 = bf16[3584,512]{1,0:T(8,128)(2,1)} fusion(bf16[1024,3584]{1,0:T(8,128)(2,1)} %constant_dynamic-update-slice_fusion, bf16[1024,1024]{1,0:T(8,128)(2,1)S(1)} %pad_maximum_fusion.2), kind=kOutput, calls=%fused_computation.10 | convolution fusion | flops 3759931392 | bytes 12058624 | tf_op jit(solution)/shard_map/dot_general | solution.py:179
  392.3 10.4 %collective-permute-done.18 = bf16[2,64,3584]{2,1,0:T(8,128)(2,1)S(1)} collective-permute-done((bf16[2,64,3584]{2,1,0:T(8,128)(2,1)S(1)}, bf16[2,64,3584]{2,1,0:T(8,128)(2,1)S(1)}, u32[]{:S(2)}, u32[]{:S(2)}) %collective-permute-start.18) | collective-permute-done | bytes 917536 | tf_op jit(solution)/shard_map/ppermute | solution.py:112
  402.9 25.5 %collective-permute-done.14 = bf16[2,64,3584]{2,1,0:T(8,128)(2,1)S(1)} collective-permute-done((bf16[2,64,3584]{2,1,0:T(8,128)(2,1)S(1)}, bf16[2,64,3584]{2,1,0:T(8,128)(2,1)S(1)}, u32[]{:S(2)}, u32[]{:S(2)}) %collective-permute-start.14) | collective-permute-done | bytes 917536 | tf_op jit(solution)/shard_map/ppermute | solution.py:112
  429.2 12.3 %collective-permute-done.43 = bf16[64,3584]{1,0:T(8,128)(2,1)S(1)} collective-permute-done((bf16[64,3584]{1,0:T(8,128)(2,1)S(1)}, bf16[64,3584]{1,0:T(8,128)(2,1)S(1)}, u32[]{:S(2)}, u32[]{:S(2)}) %collective-permute-start.43) | collective-permute-done | bytes 458784 | tf_op jit(solution)/shard_map/ppermute | solution.py:112
  445.5 17.4 %collective-permute-done.55 = bf16[64,3584]{1,0:T(8,128)(2,1)S(1)} collective-permute-done((bf16[64,3584]{1,0:T(8,128)(2,1)S(1)}, bf16[64,3584]{1,0:T(8,128)(2,1)S(1)}, u32[]{:S(2)}, u32[]{:S(2)}) %collective-permute-start.55) | collective-permute-done | bytes 458784 | tf_op jit(solution)/shard_map/ppermute | solution.py:116
  465.3 12.5 %collective-permute-done.27 = bf16[64,3584]{1,0:T(8,128)(2,1)S(1)} collective-permute-done((bf16[64,3584]{1,0:T(8,128)(2,1)S(1)}, bf16[64,3584]{1,0:T(8,128)(2,1)S(1)}, u32[]{:S(2)}, u32[]{:S(2)}) %collective-permute-start.27) | collective-permute-done | bytes 458784 | tf_op jit(solution)/shard_map/ppermute | solution.py:116
  479.1 4.6 collective-permute-start.56
  484.5 3.7 collective-permute-done.53
  489.5 2.4 collective-permute-done.56
  491.9 2.2 collective-permute-start.28
  495.6 2.9 collective-permute-done.25
  502.3 2.2 collective-permute-start.57
  505.5 3.5 collective-permute-done.54
  512.7 2.2 collective-permute-start.29
  514.8 2.1 add_convert_fusion.2
  516.9 2.4 collective-permute-done.26
  519.3 3.7 collective-permute-done.29
  523.0 2.1 add_convert_fusion.9
  525.1 8.9 %fusion = bf16[1,3584,512]{2,1,0:T(8,128)(2,1)} fusion(bf16[3584,512]{1,0:T(8,128)(2,1)S(1)} %collective-permute-done.58, bf16[1024,3584]{1,0:T(8,128)(2,1)} %constant_dynamic-update-slice_fusion, bf16[1024,1024]{1,0:T(8,128)(2,1)S(1)} %pad_maximum_fusion.2), kind=kOutput, calls=%fused_computation.11 | convolution fusion | flops 3763601408 | bytes 15728640 | tf_op jit(solution)/shard_map/dot_general | solution.py:179
  534.0 8.7 %fusion.1 = bf16[1,512,3584]{2,1,0:T(8,128)(2,1)} fusion(bf16[512,3584]{1,0:T(8,128)(2,1)S(1)} %collective-permute-done.59, bf16[1024,3584]{1,0:T(8,128)(2,1)} %constant_dynamic-update-slice_fusion.16, bf16[1024,1024]{1,0:T(8,128)(2,1)S(1)} %pad_maximum_fusion.3), kind=kOutput, calls=%fused_computation.12 | convolution fusion | flops 3763601408 | bytes 15728640 | tf_op jit(solution)/shard_map/dot_general | solution.py:179
  (280 shorter events, 101.6 us)
Async XLA Ops:
  0.6 62.7 %collective-permute-start.6 = (bf16[64,3584]{1,0:T(8,128)(2,1)}, bf16[64,3584]{1,0:T(8,128)(2,1)S(1)}, u32[]{:S(2)}, u32[]{:S(2)}) collective-permute-start(bf16[64,3584]{1,0:T(8,128)(2,1)} %param.6), channel_id=1, source_target_pairs={{24,16},{26,18},{28,20},{30,22},{16,8},{18,10},{20,12},{22,14},{8,... | collective-permute-start | bytes 1376264 | tf_op jit(solution)/shard_map/ppermute | solution.py:116
  3.1 12.3 %collective-permute-start = (bf16[64,3584]{1,0:T(8,128)(2,1)}, bf16[64,3584]{1,0:T(8,128)(2,1)S(1)}, u32[]{:S(2)}, u32[]{:S(2)}) collective-permute-start(bf16[64,3584]{1,0:T(8,128)(2,1)} %param.6), channel_id=1, source_target_pairs={{0,2},{2,0},{4,6},{6,4},{8,10},{10,8},{12,14},{14,12},{16,18},{18,... | collective-permute-start | bytes 1376264 | tf_op jit(solution)/shard_map/ppermute | solution.py:112
  4.7 59.2 %collective-permute-start.9 = (bf16[64,3584]{1,0:T(8,128)(2,1)}, bf16[64,3584]{1,0:T(8,128)(2,1)S(1)}, u32[]{:S(2)}, u32[]{:S(2)}) collective-permute-start(bf16[64,3584]{1,0:T(8,128)(2,1)} %param.6), channel_id=1, source_target_pairs={{0,8},{2,10},{4,12},{6,14},{8,16},{10,18},{12,20},{14,22},{16,24},... | collective-permute-start | bytes 1376264 | tf_op jit(solution)/shard_map/ppermute | solution.py:116
  8.2 60.5 %collective-permute-start.34 = (bf16[64,3584]{1,0:T(8,128)(2,1)}, bf16[64,3584]{1,0:T(8,128)(2,1)S(1)}, u32[]{:S(2)}, u32[]{:S(2)}) collective-permute-start(bf16[64,3584]{1,0:T(8,128)(2,1)} %param.9), channel_id=1, source_target_pairs={{24,16},{26,18},{28,20},{30,22},{16,8},{18,10},{20,12},{22,14},{8,... | collective-permute-start | bytes 1376264 | tf_op jit(solution)/shard_map/ppermute | solution.py:116
  10.5 13.7 %collective-permute-start.30 = (bf16[64,3584]{1,0:T(8,128)(2,1)}, bf16[64,3584]{1,0:T(8,128)(2,1)S(1)}, u32[]{:S(2)}, u32[]{:S(2)}) collective-permute-start(bf16[64,3584]{1,0:T(8,128)(2,1)} %param.9), channel_id=1, source_target_pairs={{0,4},{2,6},{4,0},{6,2},{8,12},{10,14},{12,8},{14,10},{16,20},{18,... | collective-permute-start | bytes 1376264 | tf_op jit(solution)/shard_map/ppermute | solution.py:112
  13.3 48.4 %copy-start.31 = (bf16[1,3584,512]{2,1,0:T(8,128)(2,1)S(1)}, bf16[1,3584,512]{2,1,0:T(8,128)(2,1)}, u32[]{:S(2)}) copy-start(bf16[1,3584,512]{2,1,0:T(8,128)(2,1)} %param.10) | copy-start | bytes 11010052
  16.5 25.1 %collective-permute-start.1 = (bf16[2,64,3584]{2,1,0:T(8,128)(2,1)S(1)}, bf16[2,64,3584]{2,1,0:T(8,128)(2,1)S(1)}, u32[]{:S(2)}, u32[]{:S(2)}) collective-permute-start(bf16[2,64,3584]{2,1,0:T(8,128)(2,1)S(1)} %pad_maximum_fusion.4), channel_id=1, source_target_pairs={{0,4},{2,6},{4,0},{6,2},{8,12},{10,14},{12,8},{14,10},{16,20},{18,... | collective-permute-start | bytes 2752520 | tf_op jit(solution)/shard_map/ppermute | solution.py:112
  24.3 45.0 %collective-permute-start.37 = (bf16[64,3584]{1,0:T(8,128)(2,1)S(1)}, bf16[64,3584]{1,0:T(8,128)(2,1)S(1)}, u32[]{:S(2)}, u32[]{:S(2)}) collective-permute-start(bf16[64,3584]{1,0:T(8,128)(2,1)S(1)} %copy-done.1), channel_id=1, source_target_pairs={{0,8},{2,10},{4,12},{6,14},{8,16},{10,18},{12,20},{14,22},{16,24},... | collective-permute-start | bytes 1376264 | tf_op jit(solution)/shard_map/ppermute | solution.py:116
  41.6 20.0 %collective-permute-start.31 = (bf16[2,64,3584]{2,1,0:T(8,128)(2,1)S(1)}, bf16[2,64,3584]{2,1,0:T(8,128)(2,1)S(1)}, u32[]{:S(2)}, u32[]{:S(2)}) collective-permute-start(bf16[2,64,3584]{2,1,0:T(8,128)(2,1)S(1)} %pad_maximum_fusion.12), channel_id=1, source_target_pairs={{0,2},{2,0},{4,6},{6,4},{8,10},{10,8},{12,14},{14,12},{16,18},{18,... | collective-permute-start | bytes 2752520 | tf_op jit(solution)/shard_map/ppermute | solution.py:112
  61.7 97.5 %collective-permute-start.2 = (bf16[3584,512]{1,0:T(8,128)(2,1)S(1)}, bf16[3584,512]{1,0:T(8,128)(2,1)S(1)}, u32[]{:S(2)}, u32[]{:S(2)}) collective-permute-start(bf16[3584,512]{1,0:T(8,128)(2,1)S(1)} %bitcast.284), channel_id=1, source_target_pairs={{0,1},{1,0},{2,3},{3,2},{4,5},{5,4},{6,7},{7,6},{8,9},{9,8},{10,11... | collective-permute-start | bytes 11010056 | tf_op jit(solution)/shard_map/ppermute | solution.py:207
  63.3 103.4 %collective-permute-start.3 = (bf16[512,3584]{1,0:T(8,128)(2,1)S(1)}, bf16[512,3584]{1,0:T(8,128)(2,1)S(1)}, u32[]{:S(2)}, u32[]{:S(2)}) collective-permute-start(bf16[512,3584]{1,0:T(8,128)(2,1)S(1)} %bitcast.293), channel_id=1, source_target_pairs={{0,1},{1,0},{2,3},{3,2},{4,5},{5,4},{6,7},{7,6},{8,9},{9,8},{10,11... | collective-permute-start | bytes 11010056 | tf_op jit(solution)/shard_map/ppermute | solution.py:208
  63.9 63.0 %collective-permute-start.7 = (bf16[64,3584]{1,0:T(8,128)(2,1)S(1)}, bf16[64,3584]{1,0:T(8,128)(2,1)}, u32[]{:S(2)}, u32[]{:S(2)}) collective-permute-start(bf16[64,3584]{1,0:T(8,128)(2,1)S(1)} %collective-permute-done.6), channel_id=1, source_target_pairs={{16,8},{18,10},{20,12},{22,14},{8,0},{10,2},{12,4},{14,6},{17,9},{... | collective-permute-start | bytes 1376264 | tf_op jit(solution)/shard_map/ppermute | solution.py:116
  68.7 53.7 %copy-start.10 = (bf16[64,3584]{1,0:T(8,128)(2,1)}, bf16[64,3584]{1,0:T(8,128)(2,1)S(1)}, u32[]{:S(2)}) copy-start(bf16[64,3584]{1,0:T(8,128)(2,1)S(1)} %collective-permute-done.34) | copy-start | bytes 1376260
  68.7 12.2 %collective-permute-start.16 = (bf16[64,3584]{1,0:T(8,128)(2,1)S(1)}, bf16[64,3584]{1,0:T(8,128)(2,1)S(1)}, u32[]{:S(2)}, u32[]{:S(2)}) collective-permute-start(bf16[64,3584]{1,0:T(8,128)(2,1)S(1)} %get-tuple-element.18), channel_id=1, source_target_pairs={{0,2},{2,0},{4,6},{6,4},{8,10},{10,8},{12,14},{14,12},{16,18},{18,... | collective-permute-start | bytes 1376264 | tf_op jit(solution)/shard_map/ppermute | solution.py:112
  69.3 57.6 %copy-start.16 = (bf16[64,3584]{1,0:T(8,128)(2,1)}, bf16[64,3584]{1,0:T(8,128)(2,1)S(1)}, u32[]{:S(2)}) copy-start(bf16[64,3584]{1,0:T(8,128)(2,1)S(1)} %collective-permute-done.37) | copy-start | bytes 1376260
  70.2 12.2 %collective-permute-start.44 = (bf16[64,3584]{1,0:T(8,128)(2,1)S(1)}, bf16[64,3584]{1,0:T(8,128)(2,1)S(1)}, u32[]{:S(2)}, u32[]{:S(2)}) collective-permute-start(bf16[64,3584]{1,0:T(8,128)(2,1)S(1)} %get-tuple-element.12), channel_id=1, source_target_pairs={{0,4},{2,6},{4,0},{6,2},{8,12},{10,14},{12,8},{14,10},{16,20},{18,... | collective-permute-start | bytes 1376264 | tf_op jit(solution)/shard_map/ppermute | solution.py:112
  81.0 21.2 %collective-permute-start.17 = (bf16[2,64,3584]{2,1,0:T(8,128)(2,1)S(1)}, bf16[2,64,3584]{2,1,0:T(8,128)(2,1)S(1)}, u32[]{:S(2)}, u32[]{:S(2)}) collective-permute-start(bf16[2,64,3584]{2,1,0:T(8,128)(2,1)S(1)} %pad_maximum_fusion.8), channel_id=1, source_target_pairs={{0,4},{2,6},{4,0},{6,2},{8,12},{10,14},{12,8},{14,10},{16,20},{18,... | collective-permute-start | bytes 2752520 | tf_op jit(solution)/shard_map/ppermute | solution.py:112
  82.4 46.4 %collective-permute-start.10 = (bf16[64,3584]{1,0:T(8,128)(2,1)S(1)}, bf16[64,3584]{1,0:T(8,128)(2,1)}, u32[]{:S(2)}, u32[]{:S(2)}) collective-permute-start(bf16[64,3584]{1,0:T(8,128)(2,1)S(1)} %copy-done.15), channel_id=1, source_target_pairs={{8,16},{10,18},{12,20},{14,22},{16,24},{18,26},{20,28},{22,30},{9,... | collective-permute-start | bytes 1376264 | tf_op jit(solution)/shard_map/ppermute | solution.py:116
  102.2 20.2 %collective-permute-start.45 = (bf16[2,64,3584]{2,1,0:T(8,128)(2,1)S(1)}, bf16[2,64,3584]{2,1,0:T(8,128)(2,1)S(1)}, u32[]{:S(2)}, u32[]{:S(2)}) collective-permute-start(bf16[2,64,3584]{2,1,0:T(8,128)(2,1)S(1)} %pad_maximum_fusion.16), channel_id=1, source_target_pairs={{0,2},{2,0},{4,6},{6,4},{8,10},{10,8},{12,14},{14,12},{16,18},{18,... | collective-permute-start | bytes 2752520 | tf_op jit(solution)/shard_map/ppermute | solution.py:112
  122.4 10.7 %collective-permute-start.35 = (bf16[64,3584]{1,0:T(8,128)(2,1)S(1)}, bf16[64,3584]{1,0:T(8,128)(2,1)}, u32[]{:S(2)}, u32[]{:S(2)}) collective-permute-start(bf16[64,3584]{1,0:T(8,128)(2,1)S(1)} %collective-permute-done.34), channel_id=1, source_target_pairs={{16,8},{18,10},{20,12},{22,14},{8,0},{10,2},{12,4},{14,6},{17,9},{... | collective-permute-start | bytes 1376264 | tf_op jit(solution)/shard_map/ppermute | solution.py:116
  126.9 12.9 %collective-permute-start.38 = (bf16[64,3584]{1,0:T(8,128)(2,1)S(1)}, bf16[64,3584]{1,0:T(8,128)(2,1)}, u32[]{:S(2)}, u32[]{:S(2)}) collective-permute-start(bf16[64,3584]{1,0:T(8,128)(2,1)S(1)} %collective-permute-done.37), channel_id=1, source_target_pairs={{8,16},{10,18},{12,20},{14,22},{16,24},{18,26},{20,28},{22,30},{9,... | collective-permute-start | bytes 1376264 | tf_op jit(solution)/shard_map/ppermute | solution.py:116
  128.8 54.3 %collective-permute-start.8 = (bf16[64,3584]{1,0:T(8,128)(2,1)}, bf16[64,3584]{1,0:T(8,128)(2,1)}, u32[]{:S(2)}, u32[]{:S(2)}) collective-permute-start(bf16[64,3584]{1,0:T(8,128)(2,1)} %collective-permute-done.7), channel_id=1, source_target_pairs={{8,0},{10,2},{12,4},{14,6},{9,1},{11,3},{13,5},{15,7}} | collective-permute-start | bytes 1376264 | tf_op jit(solution)/shard_map/ppermute | solution.py:116
  133.1 50.0 %collective-permute-start.11 = (bf16[64,3584]{1,0:T(8,128)(2,1)}, bf16[64,3584]{1,0:T(8,128)(2,1)}, u32[]{:S(2)}, u32[]{:S(2)}) collective-permute-start(bf16[64,3584]{1,0:T(8,128)(2,1)} %collective-permute-done.10), channel_id=1, source_target_pairs={{16,24},{18,26},{20,28},{22,30},{17,25},{19,27},{21,29},{23,31}} | collective-permute-start | bytes 1376264 | tf_op jit(solution)/shard_map/ppermute | solution.py:116
  139.8 8.5 %collective-permute-start.20 = (bf16[64,3584]{1,0:T(8,128)(2,1)S(1)}, bf16[64,3584]{1,0:T(8,128)(2,1)S(1)}, u32[]{:S(2)}, u32[]{:S(2)}) collective-permute-start(bf16[64,3584]{1,0:T(8,128)(2,1)S(1)} %get-tuple-element.16), channel_id=1, source_target_pairs={{0,2},{2,0},{4,6},{6,4},{8,10},{10,8},{12,14},{14,12},{16,18},{18,... | collective-permute-start | bytes 1376264 | tf_op jit(solution)/shard_map/ppermute | solution.py:112
  148.2 8.5 %collective-permute-start.48 = (bf16[64,3584]{1,0:T(8,128)(2,1)S(1)}, bf16[64,3584]{1,0:T(8,128)(2,1)S(1)}, u32[]{:S(2)}, u32[]{:S(2)}) collective-permute-start(bf16[64,3584]{1,0:T(8,128)(2,1)S(1)} %get-tuple-element.10), channel_id=1, source_target_pairs={{0,4},{2,6},{4,0},{6,2},{8,12},{10,14},{12,8},{14,10},{16,20},{18,... | collective-permute-start | bytes 1376264 | tf_op jit(solution)/shard_map/ppermute | solution.py:112
  156.7 46.3 %collective-permute-start.36 = (bf16[64,3584]{1,0:T(8,128)(2,1)}, bf16[64,3584]{1,0:T(8,128)(2,1)}, u32[]{:S(2)}, u32[]{:S(2)}) collective-permute-start(bf16[64,3584]{1,0:T(8,128)(2,1)} %collective-permute-done.35), channel_id=1, source_target_pairs={{8,0},{10,2},{12,4},{14,6},{9,1},{11,3},{13,5},{15,7}} | collective-permute-start | bytes 1376264 | tf_op jit(solution)/shard_map/ppermute | solution.py:116
  159.2 43.9 %collective-permute-start.39 = (bf16[64,3584]{1,0:T(8,128)(2,1)}, bf16[64,3584]{1,0:T(8,128)(2,1)}, u32[]{:S(2)}, u32[]{:S(2)}) collective-permute-start(bf16[64,3584]{1,0:T(8,128)(2,1)} %collective-permute-done.38), channel_id=1, source_target_pairs={{16,24},{18,26},{20,28},{22,30},{17,25},{19,27},{21,29},{23,31}} | collective-permute-start | bytes 1376264 | tf_op jit(solution)/shard_map/ppermute | solution.py:116
  166.7 13.8 %collective-permute-start.21 = (bf16[2,64,3584]{2,1,0:T(8,128)(2,1)}, bf16[2,64,3584]{2,1,0:T(8,128)(2,1)S(1)}, u32[]{:S(2)}, u32[]{:S(2)}) collective-permute-start(bf16[2,64,3584]{2,1,0:T(8,128)(2,1)} %pad_maximum_fusion.10), channel_id=1, source_target_pairs={{0,4},{2,6},{4,0},{6,2},{8,12},{10,14},{12,8},{14,10},{16,20},{18,... | collective-permute-start | bytes 2752520 | tf_op jit(solution)/shard_map/ppermute | solution.py:112
  180.5 18.0 %collective-permute-start.49 = (bf16[2,64,3584]{2,1,0:T(8,128)(2,1)}, bf16[2,64,3584]{2,1,0:T(8,128)(2,1)S(1)}, u32[]{:S(2)}, u32[]{:S(2)}) collective-permute-start(bf16[2,64,3584]{2,1,0:T(8,128)(2,1)} %pad_maximum_fusion.18), channel_id=1, source_target_pairs={{0,2},{2,0},{4,6},{6,4},{8,10},{10,8},{12,14},{14,12},{16,18},{18,... | collective-permute-start | bytes 2752520 | tf_op jit(solution)/shard_map/ppermute | solution.py:112
  185.5 24.3 %collective-permute-start.12 = (bf16[64,3584]{1,0:T(8,128)(2,1)}, bf16[64,3584]{1,0:T(8,128)(2,1)S(1)}, u32[]{:S(2)}, u32[]{:S(2)}) collective-permute-start(bf16[64,3584]{1,0:T(8,128)(2,1)} %get-tuple-element.14), channel_id=1, source_target_pairs={{0,2},{2,0},{4,6},{6,4},{8,10},{10,8},{12,14},{14,12},{16,18},{18,... | collective-permute-start | bytes 1376264 | tf_op jit(solution)/shard_map/ppermute | solution.py:112
  208.3 8.5 %collective-permute-start.40 = (bf16[64,3584]{1,0:T(8,128)(2,1)S(1)}, bf16[64,3584]{1,0:T(8,128)(2,1)S(1)}, u32[]{:S(2)}, u32[]{:S(2)}) collective-permute-start(bf16[64,3584]{1,0:T(8,128)(2,1)S(1)} %get-tuple-element.8), channel_id=1, source_target_pairs={{0,4},{2,6},{4,0},{6,2},{8,12},{10,14},{12,8},{14,10},{16,20},{18,... | collective-permute-start | bytes 1376264 | tf_op jit(solution)/shard_map/ppermute | solution.py:112
  211.2 15.5 %collective-permute-start.13 = (bf16[2,64,3584]{2,1,0:T(8,128)(2,1)S(1)}, bf16[2,64,3584]{2,1,0:T(8,128)(2,1)S(1)}, u32[]{:S(2)}, u32[]{:S(2)}) collective-permute-start(bf16[2,64,3584]{2,1,0:T(8,128)(2,1)S(1)} %pad_maximum_fusion.6), channel_id=1, source_target_pairs={{0,4},{2,6},{4,0},{6,2},{8,12},{10,14},{12,8},{14,10},{16,20},{18,... | collective-permute-start | bytes 2752520 | tf_op jit(solution)/shard_map/ppermute | solution.py:112
  216.9 13.8 %collective-permute-start.41 = (bf16[2,64,3584]{2,1,0:T(8,128)(2,1)S(1)}, bf16[2,64,3584]{2,1,0:T(8,128)(2,1)S(1)}, u32[]{:S(2)}, u32[]{:S(2)}) collective-permute-start(bf16[2,64,3584]{2,1,0:T(8,128)(2,1)S(1)} %pad_maximum_fusion.14), channel_id=1, source_target_pairs={{0,2},{2,0},{4,6},{6,4},{8,10},{10,8},{12,14},{14,12},{16,18},{18,... | collective-permute-start | bytes 2752520 | tf_op jit(solution)/shard_map/ppermute | solution.py:112
  316.4 66.4 %collective-permute-start.32 = (bf16[2,64,3584]{2,1,0:T(8,128)(2,1)S(1)}, bf16[2,64,3584]{2,1,0:T(8,128)(2,1)}, u32[]{:S(2)}, u32[]{:S(2)}) collective-permute-start(bf16[2,64,3584]{2,1,0:T(8,128)(2,1)S(1)} %pad_maximum_fusion.13), channel_id=1, source_target_pairs={{0,2},{2,0},{4,6},{6,4},{8,10},{10,8},{12,14},{14,12},{16,18},{18,... | collective-permute-start | bytes 2752520 | tf_op jit(solution)/shard_map/ppermute | solution.py:112
  325.2 60.8 %collective-permute-start.46 = (bf16[2,64,3584]{2,1,0:T(8,128)(2,1)}, bf16[2,64,3584]{2,1,0:T(8,128)(2,1)}, u32[]{:S(2)}, u32[]{:S(2)}) collective-permute-start(bf16[2,64,3584]{2,1,0:T(8,128)(2,1)} %pad_maximum_fusion.17), channel_id=1, source_target_pairs={{0,2},{2,0},{4,6},{6,4},{8,10},{10,8},{12,14},{14,12},{16,18},{18,... | collective-permute-start | bytes 2752520 | tf_op jit(solution)/shard_map/ppermute | solution.py:112
  339.4 47.9 %collective-permute-start.50 = (bf16[2,64,3584]{2,1,0:T(8,128)(2,1)S(1)}, bf16[2,64,3584]{2,1,0:T(8,128)(2,1)S(1)}, u32[]{:S(2)}, u32[]{:S(2)}) collective-permute-start(bf16[2,64,3584]{2,1,0:T(8,128)(2,1)S(1)} %pad_maximum_fusion.19), channel_id=1, source_target_pairs={{0,2},{2,0},{4,6},{6,4},{8,10},{10,8},{12,14},{14,12},{16,18},{18,... | collective-permute-start | bytes 2752520 | tf_op jit(solution)/shard_map/ppermute | solution.py:112
  340.1 49.3 %collective-permute-start.42 = (bf16[2,64,3584]{2,1,0:T(8,128)(2,1)S(1)}, bf16[2,64,3584]{2,1,0:T(8,128)(2,1)}, u32[]{:S(2)}, u32[]{:S(2)}) collective-permute-start(bf16[2,64,3584]{2,1,0:T(8,128)(2,1)S(1)} %pad_maximum_fusion.15), channel_id=1, source_target_pairs={{0,2},{2,0},{4,6},{6,4},{8,10},{10,8},{12,14},{14,12},{16,18},{18,... | collective-permute-start | bytes 2752520 | tf_op jit(solution)/shard_map/ppermute | solution.py:112
  346.1 44.5 %collective-permute-start.4 = (bf16[2,64,3584]{2,1,0:T(8,128)(2,1)S(1)}, bf16[2,64,3584]{2,1,0:T(8,128)(2,1)}, u32[]{:S(2)}, u32[]{:S(2)}) collective-permute-start(bf16[2,64,3584]{2,1,0:T(8,128)(2,1)S(1)} %pad_maximum_fusion.5), channel_id=1, source_target_pairs={{0,4},{2,6},{4,0},{6,2},{8,12},{10,14},{12,8},{14,10},{16,20},{18,... | collective-permute-start | bytes 2752520 | tf_op jit(solution)/shard_map/ppermute | solution.py:112
  382.8 20.0 %collective-permute-start.18 = (bf16[2,64,3584]{2,1,0:T(8,128)(2,1)S(1)}, bf16[2,64,3584]{2,1,0:T(8,128)(2,1)S(1)}, u32[]{:S(2)}, u32[]{:S(2)}) collective-permute-start(bf16[2,64,3584]{2,1,0:T(8,128)(2,1)S(1)} %pad_maximum_fusion.9), channel_id=1, source_target_pairs={{0,4},{2,6},{4,0},{6,2},{8,12},{10,14},{12,8},{14,10},{16,20},{18,... | collective-permute-start | bytes 2752520 | tf_op jit(solution)/shard_map/ppermute | solution.py:112
  386.0 42.6 %collective-permute-start.22 = (bf16[2,64,3584]{2,1,0:T(8,128)(2,1)S(1)}, bf16[2,64,3584]{2,1,0:T(8,128)(2,1)S(1)}, u32[]{:S(2)}, u32[]{:S(2)}) collective-permute-start(bf16[2,64,3584]{2,1,0:T(8,128)(2,1)S(1)} %pad_maximum_fusion.11), channel_id=1, source_target_pairs={{0,4},{2,6},{4,0},{6,2},{8,12},{10,14},{12,8},{14,10},{16,20},{18,... | collective-permute-start | bytes 2752520 | tf_op jit(solution)/shard_map/ppermute | solution.py:112
  387.3 41.1 %collective-permute-start.14 = (bf16[2,64,3584]{2,1,0:T(8,128)(2,1)S(1)}, bf16[2,64,3584]{2,1,0:T(8,128)(2,1)S(1)}, u32[]{:S(2)}, u32[]{:S(2)}) collective-permute-start(bf16[2,64,3584]{2,1,0:T(8,128)(2,1)S(1)} %pad_maximum_fusion.7), channel_id=1, source_target_pairs={{0,4},{2,6},{4,0},{6,2},{8,12},{10,14},{12,8},{14,10},{16,20},{18,... | collective-permute-start | bytes 2752520 | tf_op jit(solution)/shard_map/ppermute | solution.py:112
  389.4 135.7 %collective-permute-start.58 = (bf16[3584,512]{1,0:T(8,128)(2,1)S(1)}, bf16[3584,512]{1,0:T(8,128)(2,1)S(1)}, u32[]{:S(2)}, u32[]{:S(2)}) collective-permute-start(bf16[3584,512]{1,0:T(8,128)(2,1)S(1)} %copy-done.45), channel_id=1, source_target_pairs={{0,1},{1,0},{2,3},{3,2},{4,5},{5,4},{6,7},{7,6},{8,9},{9,8},{10,11... | collective-permute-start | bytes 11010056 | tf_op jit(solution)/shard_map/ppermute | solution.py:240
  390.6 143.3 %collective-permute-start.59 = (bf16[512,3584]{1,0:T(8,128)(2,1)}, bf16[512,3584]{1,0:T(8,128)(2,1)S(1)}, u32[]{:S(2)}, u32[]{:S(2)}) collective-permute-start(bf16[512,3584]{1,0:T(8,128)(2,1)} %convolution_convert_fusion), channel_id=1, source_target_pairs={{0,1},{1,0},{2,3},{3,2},{4,5},{5,4},{6,7},{7,6},{8,9},{9,8},{10,11... | collective-permute-start | bytes 11010056 | tf_op jit(solution)/shard_map/ppermute | solution.py:239
  392.3 72.6 %copy-start.28 = (bf16[2,64,3584]{2,1,0:T(8,128)(2,1)S(1)}, bf16[2,64,3584]{2,1,0:T(8,128)(2,1)}, u32[]{:S(2)}) copy-start(bf16[2,64,3584]{2,1,0:T(8,128)(2,1)} %copy-done.27) | copy-start | bytes 2752516
  402.8 42.1 %collective-permute-start.51 = (bf16[64,3584]{1,0:T(8,128)(2,1)S(1)}, bf16[64,3584]{1,0:T(8,128)(2,1)S(1)}, u32[]{:S(2)}, u32[]{:S(2)}) collective-permute-start(bf16[64,3584]{1,0:T(8,128)(2,1)S(1)} %fusion.102), channel_id=1, source_target_pairs={{0,4},{2,6},{4,0},{6,2},{8,12},{10,14},{12,8},{14,10},{16,20},{18,... | collective-permute-start | bytes 1376264 | tf_op jit(solution)/shard_map/ppermute | solution.py:112
  428.4 13.1 %collective-permute-start.43 = (bf16[64,3584]{1,0:T(8,128)(2,1)S(1)}, bf16[64,3584]{1,0:T(8,128)(2,1)S(1)}, u32[]{:S(2)}, u32[]{:S(2)}) collective-permute-start(bf16[64,3584]{1,0:T(8,128)(2,1)S(1)} %fusion.106), channel_id=1, source_target_pairs={{0,4},{2,6},{4,0},{6,2},{8,12},{10,14},{12,8},{14,10},{16,20},{18,... | collective-permute-start | bytes 1376264 | tf_op jit(solution)/shard_map/ppermute | solution.py:112
  428.6 15.5 %collective-permute-start.15 = (bf16[64,3584]{1,0:T(8,128)(2,1)S(1)}, bf16[64,3584]{1,0:T(8,128)(2,1)S(1)}, u32[]{:S(2)}, u32[]{:S(2)}) collective-permute-start(bf16[64,3584]{1,0:T(8,128)(2,1)S(1)} %fusion.114), channel_id=1, source_target_pairs={{0,2},{2,0},{4,6},{6,4},{8,10},{10,8},{12,14},{14,12},{16,18},{18,... | collective-permute-start | bytes 1376264 | tf_op jit(solution)/shard_map/ppermute | solution.py:112
  442.7 20.2 %collective-permute-start.55 = (bf16[64,3584]{1,0:T(8,128)(2,1)S(1)}, bf16[64,3584]{1,0:T(8,128)(2,1)S(1)}, u32[]{:S(2)}, u32[]{:S(2)}) collective-permute-start(bf16[64,3584]{1,0:T(8,128)(2,1)S(1)} %add_convert_fusion.7), channel_id=1, source_target_pairs={{24,16},{26,18},{28,20},{30,22},{25,17},{27,19},{29,21},{31,23}} | collective-permute-start | bytes 1376264 | tf_op jit(solution)/shard_map/ppermute | solution.py:116
  444.0 20.2 %collective-permute-start.52 = (bf16[64,3584]{1,0:T(8,128)(2,1)S(1)}, bf16[64,3584]{1,0:T(8,128)(2,1)S(1)}, u32[]{:S(2)}, u32[]{:S(2)}) collective-permute-start(bf16[64,3584]{1,0:T(8,128)(2,1)S(1)} %add_convert_fusion.7), channel_id=1, source_target_pairs={{0,8},{2,10},{4,12},{6,14},{1,9},{3,11},{5,13},{7,15}} | collective-permute-start | bytes 1376264 | tf_op jit(solution)/shard_map/ppermute | solution.py:116
  444.9 20.3 %collective-permute-start.23 = (bf16[64,3584]{1,0:T(8,128)(2,1)S(1)}, bf16[64,3584]{1,0:T(8,128)(2,1)S(1)}, u32[]{:S(2)}, u32[]{:S(2)}) collective-permute-start(bf16[64,3584]{1,0:T(8,128)(2,1)S(1)} %fusion.110), channel_id=1, source_target_pairs={{0,2},{2,0},{4,6},{6,4},{8,10},{10,8},{12,14},{14,12},{16,18},{18,... | collective-permute-start | bytes 1376264 | tf_op jit(solution)/shard_map/ppermute | solution.py:112
  462.9 14.9 %collective-permute-start.27 = (bf16[64,3584]{1,0:T(8,128)(2,1)S(1)}, bf16[64,3584]{1,0:T(8,128)(2,1)S(1)}, u32[]{:S(2)}, u32[]{:S(2)}) collective-permute-start(bf16[64,3584]{1,0:T(8,128)(2,1)S(1)} %add_convert_fusion.14), channel_id=1, source_target_pairs={{24,16},{26,18},{28,20},{30,22},{25,17},{27,19},{29,21},{31,23}} | collective-permute-start | bytes 1376264 | tf_op jit(solution)/shard_map/ppermute | solution.py:116
  464.2 14.9 %collective-permute-start.24 = (bf16[64,3584]{1,0:T(8,128)(2,1)S(1)}, bf16[64,3584]{1,0:T(8,128)(2,1)S(1)}, u32[]{:S(2)}, u32[]{:S(2)}) collective-permute-start(bf16[64,3584]{1,0:T(8,128)(2,1)S(1)} %add_convert_fusion.14), channel_id=1, source_target_pairs={{0,8},{2,10},{4,12},{6,14},{1,9},{3,11},{5,13},{7,15}} | collective-permute-start | bytes 1376264 | tf_op jit(solution)/shard_map/ppermute | solution.py:116
  465.2 18.8 %collective-permute-start.47 = (bf16[64,3584]{1,0:T(8,128)(2,1)S(1)}, bf16[64,3584]{1,0:T(8,128)(2,1)S(1)}, u32[]{:S(2)}, u32[]{:S(2)}) collective-permute-start(bf16[64,3584]{1,0:T(8,128)(2,1)S(1)} %fusion.104), channel_id=1, source_target_pairs={{0,4},{2,6},{4,0},{6,2},{8,12},{10,14},{12,8},{14,10},{16,20},{18,... | collective-permute-start | bytes 1376264 | tf_op jit(solution)/shard_map/ppermute | solution.py:112
  477.8 10.4 %collective-permute-start.53 = (bf16[64,3584]{1,0:T(8,128)(2,1)S(1)}, bf16[64,3584]{1,0:T(8,128)(2,1)S(1)}, u32[]{:S(2)}, u32[]{:S(2)}) collective-permute-start(bf16[64,3584]{1,0:T(8,128)(2,1)S(1)} %get-tuple-element.23), channel_id=1, source_target_pairs={{0,8},{2,10},{4,12},{6,14},{8,16},{10,18},{12,20},{14,22},{1,9},{3... | collective-permute-start | bytes 1376264 | tf_op jit(solution)/shard_map/ppermute | solution.py:116
  479.1 12.8 %collective-permute-start.56 = (bf16[64,3584]{1,0:T(8,128)(2,1)S(1)}, bf16[64,3584]{1,0:T(8,128)(2,1)S(1)}, u32[]{:S(2)}, u32[]{:S(2)}) collective-permute-start(bf16[64,3584]{1,0:T(8,128)(2,1)S(1)} %get-tuple-element.24), channel_id=1, source_target_pairs={{24,16},{26,18},{28,20},{30,22},{16,8},{18,10},{20,12},{22,14},{25... | collective-permute-start | bytes 1376264 | tf_op jit(solution)/shard_map/ppermute | solution.py:116
  484.0 11.5 %collective-permute-start.19 = (bf16[64,3584]{1,0:T(8,128)(2,1)S(1)}, bf16[64,3584]{1,0:T(8,128)(2,1)S(1)}, u32[]{:S(2)}, u32[]{:S(2)}) collective-permute-start(bf16[64,3584]{1,0:T(8,128)(2,1)S(1)} %fusion.112), channel_id=1, source_target_pairs={{0,2},{2,0},{4,6},{6,4},{8,10},{10,8},{12,14},{14,12},{16,18},{18,... | collective-permute-start | bytes 1376264 | tf_op jit(solution)/shard_map/ppermute | solution.py:112
  488.2 10.4 %collective-permute-start.25 = (bf16[64,3584]{1,0:T(8,128)(2,1)S(1)}, bf16[64,3584]{1,0:T(8,128)(2,1)S(1)}, u32[]{:S(2)}, u32[]{:S(2)}) collective-permute-start(bf16[64,3584]{1,0:T(8,128)(2,1)S(1)} %get-tuple-element.25), channel_id=1, source_target_pairs={{0,8},{2,10},{4,12},{6,14},{8,16},{10,18},{12,20},{14,22},{1,9},{3... | collective-permute-start | bytes 1376264 | tf_op jit(solution)/shard_map/ppermute | solution.py:116
  491.9 10.4 %collective-permute-start.28 = (bf16[64,3584]{1,0:T(8,128)(2,1)S(1)}, bf16[64,3584]{1,0:T(8,128)(2,1)S(1)}, u32[]{:S(2)}, u32[]{:S(2)}) collective-permute-start(bf16[64,3584]{1,0:T(8,128)(2,1)S(1)} %get-tuple-element.26), channel_id=1, source_target_pairs={{24,16},{26,18},{28,20},{30,22},{16,8},{18,10},{20,12},{22,14},{25... | collective-permute-start | bytes 1376264 | tf_op jit(solution)/shard_map/ppermute | solution.py:116
  495.6 9.4 %collective-permute-start.33 = (bf16[64,3584]{1,0:T(8,128)(2,1)S(1)}, bf16[64,3584]{1,0:T(8,128)(2,1)S(1)}, u32[]{:S(2)}, u32[]{:S(2)}) collective-permute-start(bf16[64,3584]{1,0:T(8,128)(2,1)S(1)} %fusion.108), channel_id=1, source_target_pairs={{0,4},{2,6},{4,0},{6,2},{8,12},{10,14},{12,8},{14,10},{16,20},{18,... | collective-permute-start | bytes 1376264 | tf_op jit(solution)/shard_map/ppermute | solution.py:112
  498.6 10.4 %collective-permute-start.54 = (bf16[64,3584]{1,0:T(8,128)(2,1)S(1)}, bf16[64,3584]{1,0:T(8,128)(2,1)S(1)}, u32[]{:S(2)}, u32[]{:S(2)}) collective-permute-start(bf16[64,3584]{1,0:T(8,128)(2,1)S(1)} %get-tuple-element.19), channel_id=1, source_target_pairs={{0,8},{2,10},{4,12},{6,14},{8,16},{10,18},{12,20},{14,22},{16,24},... | collective-permute-start | bytes 1376264 | tf_op jit(solution)/shard_map/ppermute | solution.py:116
  502.3 10.4 %collective-permute-start.57 = (bf16[64,3584]{1,0:T(8,128)(2,1)S(1)}, bf16[64,3584]{1,0:T(8,128)(2,1)S(1)}, u32[]{:S(2)}, u32[]{:S(2)}) collective-permute-start(bf16[64,3584]{1,0:T(8,128)(2,1)S(1)} %get-tuple-element.20), channel_id=1, source_target_pairs={{24,16},{26,18},{28,20},{30,22},{16,8},{18,10},{20,12},{22,14},{8,... | collective-permute-start | bytes 1376264 | tf_op jit(solution)/shard_map/ppermute | solution.py:116
  504.9 12.0 %collective-permute-start.5 = (bf16[64,3584]{1,0:T(8,128)(2,1)S(1)}, bf16[64,3584]{1,0:T(8,128)(2,1)S(1)}, u32[]{:S(2)}, u32[]{:S(2)}) collective-permute-start(bf16[64,3584]{1,0:T(8,128)(2,1)S(1)} %fusion.116), channel_id=1, source_target_pairs={{0,2},{2,0},{4,6},{6,4},{8,10},{10,8},{12,14},{14,12},{16,18},{18,... | collective-permute-start | bytes 1376264 | tf_op jit(solution)/shard_map/ppermute | solution.py:112
  508.9 10.4 %collective-permute-start.26 = (bf16[64,3584]{1,0:T(8,128)(2,1)S(1)}, bf16[64,3584]{1,0:T(8,128)(2,1)S(1)}, u32[]{:S(2)}, u32[]{:S(2)}) collective-permute-start(bf16[64,3584]{1,0:T(8,128)(2,1)S(1)} %get-tuple-element.21), channel_id=1, source_target_pairs={{0,8},{2,10},{4,12},{6,14},{8,16},{10,18},{12,20},{14,22},{16,24},... | collective-permute-start | bytes 1376264 | tf_op jit(solution)/shard_map/ppermute | solution.py:116
  512.7 10.4 %collective-permute-start.29 = (bf16[64,3584]{1,0:T(8,128)(2,1)S(1)}, bf16[64,3584]{1,0:T(8,128)(2,1)S(1)}, u32[]{:S(2)}, u32[]{:S(2)}) collective-permute-start(bf16[64,3584]{1,0:T(8,128)(2,1)S(1)} %get-tuple-element.22), channel_id=1, source_target_pairs={{24,16},{26,18},{28,20},{30,22},{16,8},{18,10},{20,12},{22,14},{8,... | collective-permute-start | bytes 1376264 | tf_op jit(solution)/shard_map/ppermute | solution.py:116
  (42 other events, 451.8 us)
where the time goes:
time: 548 us; the launch traced here: 543 us
  waiting for transfers between devices  226 us (41%)
  matrix products  101 us (18%)
  starting transfers between devices  82.1 us (15%)
  blocking collectives  67 us (12%)
  other arithmetic  35.1 us (6%)
  local copies, waits for them, and re-layouts  30.5 us (6%)
    ppermute x32, waiting for transfers between devices, swapped(): lax.ppermute(array, 'expert', tuple(((i, i ^ bit) for i in range(16))))  169 us
    ppermute x24, waiting for transfers between devices, shifted(): lax.ppermute(array, 'expert', tuple(((i, i + 4 * step) for z in senders f...  56.8 us
    ppermute x24, starting transfers between devices, shifted(): lax.ppermute(array, 'expert', tuple(((i, i + 4 * step) for z in senders f...  53.6 us
    dot_general x8, matrix products, transposed_dot(): lax.dot_general(rows, weights, (((1,), (1,)), ((), ())), preferred_elemen...  36.7 us
    dot_general x4, matrix products, outer(): lax.dot_general(rows, columns, (((0,), (0,)), ((), ())), preferred_elemen...  34.7 us
    all_gather x1, blocking collectives, dense_shards(): lax.all_gather(inner, 'expert', axis=0, tiled=True)  33.8 us
    all_gather x1, blocking collectives, dense_shards(): lax.all_gather(gate_of, 'expert', axis=0, tiled=True)  33.2 us
    ppermute x32, starting transfers between devices, swapped(): lax.ppermute(array, 'expert', tuple(((i, i ^ bit) for i in range(16))))  27.2 us
  transfers between devices with their start and end apart: 60, of which 27 were waited for; matrix products, arithmetic and copies ran while one was open for 25% of the time, Pallas kernels for 0%

commit v1 on v0

--- a/solution.py
+++ b/solution.py
@@ -5,6 +5,18 @@
 
 GELU_C = 0.7978845608028654
 GELU_A = 0.044715
+
+
+def doubled_up(x, axis, dim):
+    ways, here = (lax.axis_size(axis), lax.axis_index(axis))
+    grown, reach = (x, 1)
+    while reach < ways:
+        theirs = lax.ppermute(grown, axis, [(d, d ^ reach) for d in range(ways)])
+        mine_first = jnp.concatenate([grown, theirs], axis=dim)
+        theirs_first = jnp.concatenate([theirs, grown], axis=dim)
+        grown = jnp.where(here & reach == 0, mine_first, theirs_first)
+        reach = 2 * reach
+    return grown
 
 
 def gelu_value(hidden):
@@ -225,9 +237,7 @@
     d_tokens = scattered_layers(dx_columns, layer)
     order = jnp.concatenate(sources)
     inner = jnp.zeros((owners, tok_rows), jnp.float32).at[order].set(jnp.concatenate(inners))
-    inner_all = lax.all_gather(inner, "expert", axis=0, tiled=True).reshape(
-        owners, owners, tok_rows
-    )
+    inner_all = doubled_up(inner, "expert", 0).reshape(owners, owners, tok_rows)
     home = lax.dynamic_index_in_dim(inner_all, mine, axis=1, keepdims=False)
     d_gates = jnp.sum(jnp.where(named, home.T[:, None, :], 0.0), axis=2)
     all_x, all_u = (jnp.concatenate(slots_x), jnp.concatenate(slots_u))

time: 548 us -> 525 us (0.958)
  blocking collectives: 67 us -> 33.3 us
  waiting for transfers between devices: 226 us -> 235 us
  starting transfers between devices: 82.1 us -> 91 us
  other arithmetic: 35.1 us -> 28.8 us
    all_gather x1 -> x0, blocking collectives: 33.8 us -> none  [dense_shards(): lax.all_gather(inner, 'expert', axis=0, tiled=True)]
    ppermute x0 -> x4, starting transfers between devices: none -> 7.23 us  [doubled_up(): theirs = lax.ppermute(grown, axis, [(d, d ^ reach) for d in range(ways)])]
    ppermute x32, waiting for transfers between devices: 169 us -> 176 us  [swapped(): lax.ppermute(array, 'expert', tuple(((i, i ^ bit) for i in range(16))))]
    ppermute x0 -> x4, waiting for transfers between devices: none -> 6.55 us  [doubled_up(): theirs = lax.ppermute(grown, axis, [(d, d ^ reach) for d in range(ways)])]
  transfers between devices with their start and end apart: 60 -> 64, of which waited for: 27 -> 32; matrix products, arithmetic and copies ran while one was open for 25% -> 25% of each run, Pallas kernels for 0% -> 0%
where the time goes in v1:
time: 525 us; the launch traced here: 520 us
  waiting for transfers between devices  235 us (45%)
  matrix products  97.5 us (19%)
  starting transfers between devices  91 us (17%)
  blocking collectives  33.3 us (6%)
  local copies, waits for them, and re-layouts  32.6 us (6%)
  other arithmetic  28.8 us (5%)
    ppermute x32, waiting for transfers between devices, swapped(): lax.ppermute(array, 'expert', tuple(((i, i ^ bit) for i in range(16))))  176 us
    ppermute x24, starting transfers between devices, shifted(): lax.ppermute(array, 'expert', tuple(((i, i + 4 * step) for z in senders f...  54.1 us
    ppermute x24, waiting for transfers between devices, shifted(): lax.ppermute(array, 'expert', tuple(((i, i + 4 * step) for z in senders f...  52.9 us
    dot_general x8, matrix products, transposed_dot(): lax.dot_general(rows, weights, (((1,), (1,)), ((), ())), preferred_elemen...  36.5 us
    all_gather x1, blocking collectives, dense_shards(): lax.all_gather(gate_of, 'expert', axis=0, tiled=True)  33.3 us
    dot_general x4, matrix products, outer(): lax.dot_general(rows, columns, (((0,), (0,)), ((), ())), preferred_elemen...  32.9 us
    ppermute x32, starting transfers between devices, swapped(): lax.ppermute(array, 'expert', tuple(((i, i ^ bit) for i in range(16))))  28.5 us
    unnamed x116, local copies, waits for them, and re-layouts  26 us
  transfers between devices with their start and end apart: 64, of which 32 were waited for; matrix products, arithmetic and copies ran while one was open for 25% of the time, Pallas kernels for 0%

profile of v1, /device:TPU:20, one launch (start us, length us, event | category | flops | bytes accessed | tf_op | source)
XLA Modules:
  0.0 520.4 jit_solution(13407256813020518131)
XLA Ops:
  0.6 2.5 collective-permute-start.6
  4.7 3.5 collective-permute-start.9
  8.2 2.3 collective-permute-start.34
  18.8 5.5 %collective-permute-done.30 = bf16[64,3584]{1,0:T(8,128)(2,1)S(1)} collective-permute-done((bf16[64,3584]{1,0:T(8,128)(2,1)}, bf16[64,3584]{1,0:T(8,128)(2,1)S(1)}, u32[]{:S(2)}, u32[]{:S(2)}) %collective-permute-start.30) | collective-permute-done | bytes 458784 | tf_op jit(solution)/shard_map/ppermute | solution.py:124
  24.3 3.5 collective-permute-start.37
  27.9 13.7 %collective-permute-done.1 = bf16[2,64,3584]{2,1,0:T(8,128)(2,1)S(1)} collective-permute-done((bf16[2,64,3584]{2,1,0:T(8,128)(2,1)S(1)}, bf16[2,64,3584]{2,1,0:T(8,128)(2,1)S(1)}, u32[]{:S(2)}, u32[]{:S(2)}) %collective-permute-start.1) | collective-permute-done | bytes 917536 | tf_op jit(solution)/shard_map/ppermute | solution.py:124
  43.8 17.9 %collective-permute-done.31 = bf16[2,64,3584]{2,1,0:T(8,128)(2,1)S(1)} collective-permute-done((bf16[2,64,3584]{2,1,0:T(8,128)(2,1)S(1)}, bf16[2,64,3584]{2,1,0:T(8,128)(2,1)S(1)}, u32[]{:S(2)}, u32[]{:S(2)}) %collective-permute-start.31) | collective-permute-done | bytes 917536 | tf_op jit(solution)/shard_map/ppermute | solution.py:124
  63.9 3.2 collective-permute-start.7
  70.9 9.9 %collective-permute-done.16 = bf16[64,3584]{1,0:T(8,128)(2,1)S(1)} collective-permute-done((bf16[64,3584]{1,0:T(8,128)(2,1)S(1)}, bf16[64,3584]{1,0:T(8,128)(2,1)S(1)}, u32[]{:S(2)}, u32[]{:S(2)}) %collective-permute-start.16) | collective-permute-done | bytes 458784 | tf_op jit(solution)/shard_map/ppermute | solution.py:124
  82.4 2.1 collective-permute-start.10
  84.6 17.6 %collective-permute-done.17 = bf16[2,64,3584]{2,1,0:T(8,128)(2,1)S(1)} collective-permute-done((bf16[2,64,3584]{2,1,0:T(8,128)(2,1)S(1)}, bf16[2,64,3584]{2,1,0:T(8,128)(2,1)S(1)}, u32[]{:S(2)}, u32[]{:S(2)}) %collective-permute-start.17) | collective-permute-done | bytes 917536 | tf_op jit(solution)/shard_map/ppermute | solution.py:124
  104.9 17.5 %collective-permute-done.45 = bf16[2,64,3584]{2,1,0:T(8,128)(2,1)S(1)} collective-permute-done((bf16[2,64,3584]{2,1,0:T(8,128)(2,1)S(1)}, bf16[2,64,3584]{2,1,0:T(8,128)(2,1)S(1)}, u32[]{:S(2)}, u32[]{:S(2)}) %collective-permute-start.45) | collective-permute-done | bytes 917536 | tf_op jit(solution)/shard_map/ppermute | solution.py:124
  122.4 2.8 collective-permute-start.35
  133.0 2.1 collective-permute-start.11
  135.1 4.6 collective-permute-done.38
  143.6 4.6 collective-permute-done.20
  150.5 6.1 %collective-permute-done.48 = bf16[64,3584]{1,0:T(8,128)(2,1)S(1)} collective-permute-done((bf16[64,3584]{1,0:T(8,128)(2,1)S(1)}, bf16[64,3584]{1,0:T(8,128)(2,1)S(1)}, u32[]{:S(2)}, u32[]{:S(2)}) %collective-permute-start.48) | collective-permute-done | bytes 458784 | tf_op jit(solution)/shard_map/ppermute | solution.py:124
  159.1 5.4 %collective-permute-start.39 = (bf16[64,3584]{1,0:T(8,128)(2,1)}, bf16[64,3584]{1,0:T(8,128)(2,1)}, u32[]{:S(2)}, u32[]{:S(2)}) collective-permute-start(bf16[64,3584]{1,0:T(8,128)(2,1)} %collective-permute-done.38), channel_id=1, source_target_pairs={{16,24},{18,26},{20,28},{22,30},{17,25},{19,27},{21,29},{23,31}} | collective-permute-start | bytes 1376264 | tf_op jit(solution)/shard_map/ppermute | solution.py:128
  167.2 3.2 multiply_reduce_fusion.3
  170.4 3.0 fusion.18
  173.6 6.6 %multiply_reduce_fusion.2 = (f32[256]{0:T(256)S(1)}, f32[256,1024]{1,0:T(8,128)}) fusion(f32[256,1024]{1,0:T(8,128)} %fusion.18, bf16[512,3584]{1,0:T(8,128)(2,1)} %copy-done.37, bf16[512,3584]{1,0:T(8,128)(2,1)} %bitcast.293, bf16[64,3584]{1,0:T(8,128)(2,1)} %get-tuple-element.58, bf16[64,3584]{1,0:T(8,128)(2,1)S(1)} %collective-permute-done.44, ...), kind=kOutput, calls=%fused_computation.133 | convolution fusion | flops 1903689472 | bytes 11273216 | tf_op jit(solution)/shard_map/dot_general | solution.py:185
  183.1 2.3 constant_dynamic-update-slice_fusion.3
  186.4 11.8 %collective-permute-done.49 = bf16[2,64,3584]{2,1,0:T(8,128)(2,1)S(1)} collective-permute-done((bf16[2,64,3584]{2,1,0:T(8,128)(2,1)}, bf16[2,64,3584]{2,1,0:T(8,128)(2,1)S(1)}, u32[]{:S(2)}, u32[]{:S(2)}) %collective-permute-start.49) | collective-permute-done | bytes 917536 | tf_op jit(solution)/shard_map/ppermute | solution.py:124
  200.7 2.1 fusion.26
  204.8 3.2 multiply_reduce_fusion.1
  210.3 6.3 %collective-permute-done.40 = bf16[64,3584]{1,0:T(8,128)(2,1)S(1)} collective-permute-done((bf16[64,3584]{1,0:T(8,128)(2,1)S(1)}, bf16[64,3584]{1,0:T(8,128)(2,1)S(1)}, u32[]{:S(2)}, u32[]{:S(2)}) %collective-permute-start.40) | collective-permute-done | bytes 458784 | tf_op jit(solution)/shard_map/ppermute | solution.py:124
  218.8 7.5 %collective-permute-done.13 = bf16[2,64,3584]{2,1,0:T(8,128)(2,1)S(1)} collective-permute-done((bf16[2,64,3584]{2,1,0:T(8,128)(2,1)S(1)}, bf16[2,64,3584]{2,1,0:T(8,128)(2,1)S(1)}, u32[]{:S(2)}, u32[]{:S(2)}) %collective-permute-start.13) | collective-permute-done | bytes 917536 | tf_op jit(solution)/shard_map/ppermute | solution.py:124
  226.5 3.7 collective-permute-done.41
  233.6 3.6 multiply_reduce_fusion
  246.2 3.1 collective-permute-done.60
  249.3 4.3 collective-permute-start.61
  256.5 33.3 %all-gather = f32[16,64,16]{1,2,0:T(8,128)S(1)} all-gather(f32[1,64,16]{1,2,0:T(8,128)S(1)} %bitcast.280), channel_id=1, replica_groups=mesh['expert'=16,'tok'=2] {'expert'}, dimensions={0}, use_global_device_ids=true | all-gather | bytes 69632 | tf_op jit(solution)/shard_map/all_gather | solution.py:206
  292.4 2.4 fusion.78
  294.7 5.3 %convolution_convert_fusion.5 = bf16[256,3584]{1,0:T(8,128)(2,1)S(1)} fusion(bf16[256,1024]{1,0:T(8,128)(2,1)S(1)} %get-tuple-element.43, bf16[3584,512]{1,0:T(8,128)(2,1)} %copy-done.40, bf16[3584,512]{1,0:T(8,128)(2,1)} %bitcast.284), kind=kOutput, calls=%fused_computation.16 | convolution fusion | flops 1894645760 | bytes 9699328 | tf_op jit(solution)/shard_map/dot_general | solution.py:185
  302.7 4.2 convolution_convert_fusion.3
  310.1 5.3 %convolution_convert_fusion.4 = bf16[256,3584]{1,0:T(8,128)(2,1)S(1)} fusion(bf16[256,1024]{1,0:T(8,128)(2,1)S(1)} %get-tuple-element.49, bf16[3584,512]{1,0:T(8,128)(2,1)} %copy-done.40, bf16[3584,512]{1,0:T(8,128)(2,1)} %bitcast.285), kind=kOutput, calls=%fused_computation.15 | convolution fusion | flops 1894645760 | bytes 9699328 | tf_op jit(solution)/shard_map/dot_general | solution.py:185
  315.4 5.3 %convolution_convert_fusion.2 = bf16[256,3584]{1,0:T(8,128)(2,1)S(1)} fusion(bf16[256,1024]{1,0:T(8,128)(2,1)S(1)} %get-tuple-element.47, bf16[3584,512]{1,0:T(8,128)(2,1)} %copy-done.40, bf16[3584,512]{1,0:T(8,128)(2,1)} %bitcast.286), kind=kOutput, calls=%fused_computation.13 | convolution fusion | flops 1894645760 | bytes 9699328 | tf_op jit(solution)/shard_map/dot_general | solution.py:185
  323.1 4.3 convolution_convert_fusion.9
  327.6 2.3 collective-permute-start.4
  329.9 4.1 convolution_convert_fusion.7
  334.3 5.2 %convolution_convert_fusion.8 = bf16[256,3584]{1,0:T(8,128)(2,1)S(1)} fusion(bf16[256,1024]{1,0:T(8,128)(2,1)S(1)} %get-tuple-element.50, bf16[512,3584]{1,0:T(8,128)(2,1)} %copy-done.37, bf16[512,3584]{1,0:T(8,128)(2,1)} %bitcast.294), kind=kOutput, calls=%fused_computation.19 | convolution fusion | flops 1894645760 | bytes 9699328 | tf_op jit(solution)/shard_map/dot_general | solution.py:232
  339.6 5.2 %convolution_convert_fusion.6 = bf16[256,3584]{1,0:T(8,128)(2,1)S(1)} fusion(bf16[256,1024]{1,0:T(8,128)(2,1)S(1)} %get-tuple-element.48, bf16[512,3584]{1,0:T(8,128)(2,1)} %copy-done.37, bf16[512,3584]{1,0:T(8,128)(2,1)} %bitcast.295), kind=kOutput, calls=%fused_computation.17 | convolution fusion | flops 1894645760 | bytes 9699328 | tf_op jit(solution)/shard_map/dot_general | solution.py:232
  345.2 8.6 %convolution_convert_fusion = bf16[512,3584]{1,0:T(8,128)(2,1)} fusion(bf16[1024,3584]{1,0:T(8,128)(2,1)} %constant_dynamic-update-slice_fusion.16, bf16[1024,1024]{1,0:T(8,128)(2,1)S(1)} %pad_maximum_fusion.3), kind=kOutput, calls=%fused_computation.9 | convolution fusion | flops 3759931392 | bytes 12058624 | tf_op jit(solution)/shard_map/dot_general | solution.py:191
  353.8 8.6 %convolution_convert_fusion.1 = bf16[3584,512]{1,0:T(8,128)(2,1)} fusion(bf16[1024,3584]{1,0:T(8,128)(2,1)} %constant_dynamic-update-slice_fusion, bf16[1024,1024]{1,0:T(8,128)(2,1)S(1)} %pad_maximum_fusion.2), kind=kOutput, calls=%fused_computation.10 | convolution fusion | flops 3759931392 | bytes 12058624 | tf_op jit(solution)/shard_map/dot_general | solution.py:191
  362.5 2.1 collective-permute-start.22
  367.8 17.8 %collective-permute-done.18 = bf16[2,64,3584]{2,1,0:T(8,128)(2,1)S(1)} collective-permute-done((bf16[2,64,3584]{2,1,0:T(8,128)(2,1)S(1)}, bf16[2,64,3584]{2,1,0:T(8,128)(2,1)S(1)}, u32[]{:S(2)}, u32[]{:S(2)}) %collective-permute-start.18) | collective-permute-done | bytes 917536 | tf_op jit(solution)/shard_map/ppermute | solution.py:124
  385.8 24.3 %collective-permute-done.14 = bf16[2,64,3584]{2,1,0:T(8,128)(2,1)S(1)} collective-permute-done((bf16[2,64,3584]{2,1,0:T(8,128)(2,1)S(1)}, bf16[2,64,3584]{2,1,0:T(8,128)(2,1)S(1)}, u32[]{:S(2)}, u32[]{:S(2)}) %collective-permute-start.14) | collective-permute-done | bytes 917536 | tf_op jit(solution)/shard_map/ppermute | solution.py:124
  413.5 11.1 %collective-permute-done.43 = bf16[64,3584]{1,0:T(8,128)(2,1)S(1)} collective-permute-done((bf16[64,3584]{1,0:T(8,128)(2,1)S(1)}, bf16[64,3584]{1,0:T(8,128)(2,1)S(1)}, u32[]{:S(2)}, u32[]{:S(2)}) %collective-permute-start.43) | collective-permute-done | bytes 458784 | tf_op jit(solution)/shard_map/ppermute | solution.py:124
  428.5 13.1 %collective-permute-done.55 = bf16[64,3584]{1,0:T(8,128)(2,1)S(1)} collective-permute-done((bf16[64,3584]{1,0:T(8,128)(2,1)S(1)}, bf16[64,3584]{1,0:T(8,128)(2,1)S(1)}, u32[]{:S(2)}, u32[]{:S(2)}) %collective-permute-start.55) | collective-permute-done | bytes 458784 | tf_op jit(solution)/shard_map/ppermute | solution.py:128
  444.0 12.2 %collective-permute-done.27 = bf16[64,3584]{1,0:T(8,128)(2,1)S(1)} collective-permute-done((bf16[64,3584]{1,0:T(8,128)(2,1)S(1)}, bf16[64,3584]{1,0:T(8,128)(2,1)S(1)}, u32[]{:S(2)}, u32[]{:S(2)}) %collective-permute-start.27) | collective-permute-done | bytes 458784 | tf_op jit(solution)/shard_map/ppermute | solution.py:128
  457.5 4.6 collective-permute-start.56
  463.4 3.1 collective-permute-done.53
  467.8 3.2 collective-permute-done.56
  471.0 2.2 collective-permute-start.28
  474.7 2.2 collective-permute-done.25
  478.8 2.5 collective-permute-done.28
  481.3 2.5 collective-permute-start.57
  489.2 2.8 collective-permute-done.57
  492.0 2.2 collective-permute-start.29
  495.2 2.4 collective-permute-done.26
  497.6 4.7 collective-permute-done.29
  502.3 2.1 add_convert_fusion.9
  504.4 7.1 %fusion = bf16[1,3584,512]{2,1,0:T(8,128)(2,1)} fusion(bf16[3584,512]{1,0:T(8,128)(2,1)} %collective-permute-done.62, bf16[1024,3584]{1,0:T(8,128)(2,1)S(1)} %bitcast.283, bf16[1024,1024]{1,0:T(8,128)(2,1)S(1)} %pad_maximum_fusion.2), kind=kOutput, calls=%fused_computation.11 | convolution fusion | flops 3763601408 | bytes 15728640 | tf_op jit(solution)/shard_map/dot_general | solution.py:191
  511.5 8.7 %fusion.1 = bf16[1,512,3584]{2,1,0:T(8,128)(2,1)} fusion(bf16[512,3584]{1,0:T(8,128)(2,1)S(1)} %collective-permute-done.63, bf16[1024,3584]{1,0:T(8,128)(2,1)} %constant_dynamic-update-slice_fusion.16, bf16[1024,1024]{1,0:T(8,128)(2,1)S(1)} %pad_maximum_fusion.3), kind=kOutput, calls=%fused_computation.12 | convolution fusion | flops 3763601408 | bytes 15728640 | tf_op jit(solution)/shard_map/dot_general | solution.py:191
  (292 shorter events, 108.0 us)
Async XLA Ops:
  0.6 62.6 %collective-permute-start.6 = (bf16[64,3584]{1,0:T(8,128)(2,1)}, bf16[64,3584]{1,0:T(8,128)(2,1)S(1)}, u32[]{:S(2)}, u32[]{:S(2)}) collective-permute-start(bf16[64,3584]{1,0:T(8,128)(2,1)} %param.6), channel_id=1, source_target_pairs={{24,16},{26,18},{28,20},{30,22},{16,8},{18,10},{20,12},{22,14},{8,... | collective-permute-start | bytes 1376264 | tf_op jit(solution)/shard_map/ppermute | solution.py:128
  3.1 12.3 %collective-permute-start = (bf16[64,3584]{1,0:T(8,128)(2,1)}, bf16[64,3584]{1,0:T(8,128)(2,1)S(1)}, u32[]{:S(2)}, u32[]{:S(2)}) collective-permute-start(bf16[64,3584]{1,0:T(8,128)(2,1)} %param.6), channel_id=1, source_target_pairs={{0,2},{2,0},{4,6},{6,4},{8,10},{10,8},{12,14},{14,12},{16,18},{18,... | collective-permute-start | bytes 1376264 | tf_op jit(solution)/shard_map/ppermute | solution.py:124
  4.7 59.2 %collective-permute-start.9 = (bf16[64,3584]{1,0:T(8,128)(2,1)}, bf16[64,3584]{1,0:T(8,128)(2,1)S(1)}, u32[]{:S(2)}, u32[]{:S(2)}) collective-permute-start(bf16[64,3584]{1,0:T(8,128)(2,1)} %param.6), channel_id=1, source_target_pairs={{0,8},{2,10},{4,12},{6,14},{8,16},{10,18},{12,20},{14,22},{16,24},... | collective-permute-start | bytes 1376264 | tf_op jit(solution)/shard_map/ppermute | solution.py:128
  8.2 60.5 %collective-permute-start.34 = (bf16[64,3584]{1,0:T(8,128)(2,1)}, bf16[64,3584]{1,0:T(8,128)(2,1)S(1)}, u32[]{:S(2)}, u32[]{:S(2)}) collective-permute-start(bf16[64,3584]{1,0:T(8,128)(2,1)} %param.9), channel_id=1, source_target_pairs={{24,16},{26,18},{28,20},{30,22},{16,8},{18,10},{20,12},{22,14},{8,... | collective-permute-start | bytes 1376264 | tf_op jit(solution)/shard_map/ppermute | solution.py:128
  10.5 13.7 %collective-permute-start.30 = (bf16[64,3584]{1,0:T(8,128)(2,1)}, bf16[64,3584]{1,0:T(8,128)(2,1)S(1)}, u32[]{:S(2)}, u32[]{:S(2)}) collective-permute-start(bf16[64,3584]{1,0:T(8,128)(2,1)} %param.9), channel_id=1, source_target_pairs={{0,4},{2,6},{4,0},{6,2},{8,12},{10,14},{12,8},{14,10},{16,20},{18,... | collective-permute-start | bytes 1376264 | tf_op jit(solution)/shard_map/ppermute | solution.py:124
  16.5 25.1 %collective-permute-start.1 = (bf16[2,64,3584]{2,1,0:T(8,128)(2,1)S(1)}, bf16[2,64,3584]{2,1,0:T(8,128)(2,1)S(1)}, u32[]{:S(2)}, u32[]{:S(2)}) collective-permute-start(bf16[2,64,3584]{2,1,0:T(8,128)(2,1)S(1)} %pad_maximum_fusion.4), channel_id=1, source_target_pairs={{0,4},{2,6},{4,0},{6,2},{8,12},{10,14},{12,8},{14,10},{16,20},{18,... | collective-permute-start | bytes 2752520 | tf_op jit(solution)/shard_map/ppermute | solution.py:124
  24.3 45.0 %collective-permute-start.37 = (bf16[64,3584]{1,0:T(8,128)(2,1)S(1)}, bf16[64,3584]{1,0:T(8,128)(2,1)S(1)}, u32[]{:S(2)}, u32[]{:S(2)}) collective-permute-start(bf16[64,3584]{1,0:T(8,128)(2,1)S(1)} %copy-done.1), channel_id=1, source_target_pairs={{0,8},{2,10},{4,12},{6,14},{8,16},{10,18},{12,20},{14,22},{16,24},... | collective-permute-start | bytes 1376264 | tf_op jit(solution)/shard_map/ppermute | solution.py:128
  41.6 20.0 %collective-permute-start.31 = (bf16[2,64,3584]{2,1,0:T(8,128)(2,1)S(1)}, bf16[2,64,3584]{2,1,0:T(8,128)(2,1)S(1)}, u32[]{:S(2)}, u32[]{:S(2)}) collective-permute-start(bf16[2,64,3584]{2,1,0:T(8,128)(2,1)S(1)} %pad_maximum_fusion.12), channel_id=1, source_target_pairs={{0,2},{2,0},{4,6},{6,4},{8,10},{10,8},{12,14},{14,12},{16,18},{18,... | collective-permute-start | bytes 2752520 | tf_op jit(solution)/shard_map/ppermute | solution.py:124
  61.7 97.4 %collective-permute-start.2 = (bf16[3584,512]{1,0:T(8,128)(2,1)S(1)}, bf16[3584,512]{1,0:T(8,128)(2,1)S(1)}, u32[]{:S(2)}, u32[]{:S(2)}) collective-permute-start(bf16[3584,512]{1,0:T(8,128)(2,1)S(1)} %bitcast.287), channel_id=1, source_target_pairs={{0,1},{1,0},{2,3},{3,2},{4,5},{5,4},{6,7},{7,6},{8,9},{9,8},{10,11... | collective-permute-start | bytes 11010056 | tf_op jit(solution)/shard_map/ppermute | solution.py:219
  63.3 103.3 %collective-permute-start.3 = (bf16[512,3584]{1,0:T(8,128)(2,1)S(1)}, bf16[512,3584]{1,0:T(8,128)(2,1)S(1)}, u32[]{:S(2)}, u32[]{:S(2)}) collective-permute-start(bf16[512,3584]{1,0:T(8,128)(2,1)S(1)} %bitcast.296), channel_id=1, source_target_pairs={{0,1},{1,0},{2,3},{3,2},{4,5},{5,4},{6,7},{7,6},{8,9},{9,8},{10,11... | collective-permute-start | bytes 11010056 | tf_op jit(solution)/shard_map/ppermute | solution.py:220
  63.9 62.9 %collective-permute-start.7 = (bf16[64,3584]{1,0:T(8,128)(2,1)S(1)}, bf16[64,3584]{1,0:T(8,128)(2,1)}, u32[]{:S(2)}, u32[]{:S(2)}) collective-permute-start(bf16[64,3584]{1,0:T(8,128)(2,1)S(1)} %collective-permute-done.6), channel_id=1, source_target_pairs={{16,8},{18,10},{20,12},{22,14},{8,0},{10,2},{12,4},{14,6},{17,9},{... | collective-permute-start | bytes 1376264 | tf_op jit(solution)/shard_map/ppermute | solution.py:128
  68.7 12.2 %collective-permute-start.16 = (bf16[64,3584]{1,0:T(8,128)(2,1)S(1)}, bf16[64,3584]{1,0:T(8,128)(2,1)S(1)}, u32[]{:S(2)}, u32[]{:S(2)}) collective-permute-start(bf16[64,3584]{1,0:T(8,128)(2,1)S(1)} %get-tuple-element.18), channel_id=1, source_target_pairs={{0,2},{2,0},{4,6},{6,4},{8,10},{10,8},{12,14},{14,12},{16,18},{18,... | collective-permute-start | bytes 1376264 | tf_op jit(solution)/shard_map/ppermute | solution.py:124
  70.2 12.2 %collective-permute-start.44 = (bf16[64,3584]{1,0:T(8,128)(2,1)S(1)}, bf16[64,3584]{1,0:T(8,128)(2,1)S(1)}, u32[]{:S(2)}, u32[]{:S(2)}) collective-permute-start(bf16[64,3584]{1,0:T(8,128)(2,1)S(1)} %get-tuple-element.12), channel_id=1, source_target_pairs={{0,4},{2,6},{4,0},{6,2},{8,12},{10,14},{12,8},{14,10},{16,20},{18,... | collective-permute-start | bytes 1376264 | tf_op jit(solution)/shard_map/ppermute | solution.py:124
  81.0 21.2 %collective-permute-start.17 = (bf16[2,64,3584]{2,1,0:T(8,128)(2,1)S(1)}, bf16[2,64,3584]{2,1,0:T(8,128)(2,1)S(1)}, u32[]{:S(2)}, u32[]{:S(2)}) collective-permute-start(bf16[2,64,3584]{2,1,0:T(8,128)(2,1)S(1)} %pad_maximum_fusion.8), channel_id=1, source_target_pairs={{0,4},{2,6},{4,0},{6,2},{8,12},{10,14},{12,8},{14,10},{16,20},{18,... | collective-permute-start | bytes 2752520 | tf_op jit(solution)/shard_map/ppermute | solution.py:124
  82.4 46.4 %collective-permute-start.10 = (bf16[64,3584]{1,0:T(8,128)(2,1)S(1)}, bf16[64,3584]{1,0:T(8,128)(2,1)}, u32[]{:S(2)}, u32[]{:S(2)}) collective-permute-start(bf16[64,3584]{1,0:T(8,128)(2,1)S(1)} %copy-done.14), channel_id=1, source_target_pairs={{8,16},{10,18},{12,20},{14,22},{16,24},{18,26},{20,28},{22,30},{9,... | collective-permute-start | bytes 1376264 | tf_op jit(solution)/shard_map/ppermute | solution.py:128
  102.2 20.2 %collective-permute-start.45 = (bf16[2,64,3584]{2,1,0:T(8,128)(2,1)S(1)}, bf16[2,64,3584]{2,1,0:T(8,128)(2,1)S(1)}, u32[]{:S(2)}, u32[]{:S(2)}) collective-permute-start(bf16[2,64,3584]{2,1,0:T(8,128)(2,1)S(1)} %pad_maximum_fusion.16), channel_id=1, source_target_pairs={{0,2},{2,0},{4,6},{6,4},{8,10},{10,8},{12,14},{14,12},{16,18},{18,... | collective-permute-start | bytes 2752520 | tf_op jit(solution)/shard_map/ppermute | solution.py:124
  122.4 10.6 %collective-permute-start.35 = (bf16[64,3584]{1,0:T(8,128)(2,1)S(1)}, bf16[64,3584]{1,0:T(8,128)(2,1)}, u32[]{:S(2)}, u32[]{:S(2)}) collective-permute-start(bf16[64,3584]{1,0:T(8,128)(2,1)S(1)} %collective-permute-done.34), channel_id=1, source_target_pairs={{16,8},{18,10},{20,12},{22,14},{8,0},{10,2},{12,4},{14,6},{17,9},{... | collective-permute-start | bytes 1376264 | tf_op jit(solution)/shard_map/ppermute | solution.py:128
  126.8 12.9 %collective-permute-start.38 = (bf16[64,3584]{1,0:T(8,128)(2,1)S(1)}, bf16[64,3584]{1,0:T(8,128)(2,1)}, u32[]{:S(2)}, u32[]{:S(2)}) collective-permute-start(bf16[64,3584]{1,0:T(8,128)(2,1)S(1)} %collective-permute-done.37), channel_id=1, source_target_pairs={{8,16},{10,18},{12,20},{14,22},{16,24},{18,26},{20,28},{22,30},{9,... | collective-permute-start | bytes 1376264 | tf_op jit(solution)/shard_map/ppermute | solution.py:128
  128.7 54.4 %collective-permute-start.8 = (bf16[64,3584]{1,0:T(8,128)(2,1)}, bf16[64,3584]{1,0:T(8,128)(2,1)}, u32[]{:S(2)}, u32[]{:S(2)}) collective-permute-start(bf16[64,3584]{1,0:T(8,128)(2,1)} %collective-permute-done.7), channel_id=1, source_target_pairs={{8,0},{10,2},{12,4},{14,6},{9,1},{11,3},{13,5},{15,7}} | collective-permute-start | bytes 1376264 | tf_op jit(solution)/shard_map/ppermute | solution.py:128
  133.0 50.1 %collective-permute-start.11 = (bf16[64,3584]{1,0:T(8,128)(2,1)}, bf16[64,3584]{1,0:T(8,128)(2,1)}, u32[]{:S(2)}, u32[]{:S(2)}) collective-permute-start(bf16[64,3584]{1,0:T(8,128)(2,1)} %collective-permute-done.10), channel_id=1, source_target_pairs={{16,24},{18,26},{20,28},{22,30},{17,25},{19,27},{21,29},{23,31}} | collective-permute-start | bytes 1376264 | tf_op jit(solution)/shard_map/ppermute | solution.py:128
  139.7 8.5 %collective-permute-start.20 = (bf16[64,3584]{1,0:T(8,128)(2,1)S(1)}, bf16[64,3584]{1,0:T(8,128)(2,1)S(1)}, u32[]{:S(2)}, u32[]{:S(2)}) collective-permute-start(bf16[64,3584]{1,0:T(8,128)(2,1)S(1)} %get-tuple-element.16), channel_id=1, source_target_pairs={{0,2},{2,0},{4,6},{6,4},{8,10},{10,8},{12,14},{14,12},{16,18},{18,... | collective-permute-start | bytes 1376264 | tf_op jit(solution)/shard_map/ppermute | solution.py:124
  148.2 8.5 %collective-permute-start.48 = (bf16[64,3584]{1,0:T(8,128)(2,1)S(1)}, bf16[64,3584]{1,0:T(8,128)(2,1)S(1)}, u32[]{:S(2)}, u32[]{:S(2)}) collective-permute-start(bf16[64,3584]{1,0:T(8,128)(2,1)S(1)} %get-tuple-element.10), channel_id=1, source_target_pairs={{0,4},{2,6},{4,0},{6,2},{8,12},{10,14},{12,8},{14,10},{16,20},{18,... | collective-permute-start | bytes 1376264 | tf_op jit(solution)/shard_map/ppermute | solution.py:124
  156.7 46.2 %collective-permute-start.36 = (bf16[64,3584]{1,0:T(8,128)(2,1)}, bf16[64,3584]{1,0:T(8,128)(2,1)}, u32[]{:S(2)}, u32[]{:S(2)}) collective-permute-start(bf16[64,3584]{1,0:T(8,128)(2,1)} %collective-permute-done.35), channel_id=1, source_target_pairs={{8,0},{10,2},{12,4},{14,6},{9,1},{11,3},{13,5},{15,7}} | collective-permute-start | bytes 1376264 | tf_op jit(solution)/shard_map/ppermute | solution.py:128
  159.1 43.7 %collective-permute-start.39 = (bf16[64,3584]{1,0:T(8,128)(2,1)}, bf16[64,3584]{1,0:T(8,128)(2,1)}, u32[]{:S(2)}, u32[]{:S(2)}) collective-permute-start(bf16[64,3584]{1,0:T(8,128)(2,1)} %collective-permute-done.38), channel_id=1, source_target_pairs={{16,24},{18,26},{20,28},{22,30},{17,25},{19,27},{21,29},{23,31}} | collective-permute-start | bytes 1376264 | tf_op jit(solution)/shard_map/ppermute | solution.py:128
  166.6 13.7 %collective-permute-start.21 = (bf16[2,64,3584]{2,1,0:T(8,128)(2,1)}, bf16[2,64,3584]{2,1,0:T(8,128)(2,1)S(1)}, u32[]{:S(2)}, u32[]{:S(2)}) collective-permute-start(bf16[2,64,3584]{2,1,0:T(8,128)(2,1)} %pad_maximum_fusion.10), channel_id=1, source_target_pairs={{0,4},{2,6},{4,0},{6,2},{8,12},{10,14},{12,8},{14,10},{16,20},{18,... | collective-permute-start | bytes 2752520 | tf_op jit(solution)/shard_map/ppermute | solution.py:124
  180.3 17.9 %collective-permute-start.49 = (bf16[2,64,3584]{2,1,0:T(8,128)(2,1)}, bf16[2,64,3584]{2,1,0:T(8,128)(2,1)S(1)}, u32[]{:S(2)}, u32[]{:S(2)}) collective-permute-start(bf16[2,64,3584]{2,1,0:T(8,128)(2,1)} %pad_maximum_fusion.18), channel_id=1, source_target_pairs={{0,2},{2,0},{4,6},{6,4},{8,10},{10,8},{12,14},{14,12},{16,18},{18,... | collective-permute-start | bytes 2752520 | tf_op jit(solution)/shard_map/ppermute | solution.py:124
  185.4 24.2 %collective-permute-start.12 = (bf16[64,3584]{1,0:T(8,128)(2,1)S(1)}, bf16[64,3584]{1,0:T(8,128)(2,1)S(1)}, u32[]{:S(2)}, u32[]{:S(2)}) collective-permute-start(bf16[64,3584]{1,0:T(8,128)(2,1)S(1)} %get-tuple-element.14), channel_id=1, source_target_pairs={{0,2},{2,0},{4,6},{6,4},{8,10},{10,8},{12,14},{14,12},{16,18},{18,... | collective-permute-start | bytes 1376264 | tf_op jit(solution)/shard_map/ppermute | solution.py:124
  208.1 8.5 %collective-permute-start.40 = (bf16[64,3584]{1,0:T(8,128)(2,1)S(1)}, bf16[64,3584]{1,0:T(8,128)(2,1)S(1)}, u32[]{:S(2)}, u32[]{:S(2)}) collective-permute-start(bf16[64,3584]{1,0:T(8,128)(2,1)S(1)} %get-tuple-element.8), channel_id=1, source_target_pairs={{0,4},{2,6},{4,0},{6,2},{8,12},{10,14},{12,8},{14,10},{16,20},{18,... | collective-permute-start | bytes 1376264 | tf_op jit(solution)/shard_map/ppermute | solution.py:124
  209.7 16.7 %collective-permute-start.13 = (bf16[2,64,3584]{2,1,0:T(8,128)(2,1)S(1)}, bf16[2,64,3584]{2,1,0:T(8,128)(2,1)S(1)}, u32[]{:S(2)}, u32[]{:S(2)}) collective-permute-start(bf16[2,64,3584]{2,1,0:T(8,128)(2,1)S(1)} %pad_maximum_fusion.6), channel_id=1, source_target_pairs={{0,4},{2,6},{4,0},{6,2},{8,12},{10,14},{12,8},{14,10},{16,20},{18,... | collective-permute-start | bytes 2752520 | tf_op jit(solution)/shard_map/ppermute | solution.py:124
  216.6 13.5 %collective-permute-start.41 = (bf16[2,64,3584]{2,1,0:T(8,128)(2,1)S(1)}, bf16[2,64,3584]{2,1,0:T(8,128)(2,1)S(1)}, u32[]{:S(2)}, u32[]{:S(2)}) collective-permute-start(bf16[2,64,3584]{2,1,0:T(8,128)(2,1)S(1)} %pad_maximum_fusion.14), channel_id=1, source_target_pairs={{0,2},{2,0},{4,6},{6,4},{8,10},{10,8},{12,14},{14,12},{16,18},{18,... | collective-permute-start | bytes 2752520 | tf_op jit(solution)/shard_map/ppermute | solution.py:124
  237.9 3.7 collective-permute-start.58
  241.6 3.7 collective-permute-start.59
  245.3 3.9 collective-permute-start.60
  249.3 6.6 %collective-permute-start.61 = (f32[128,64]{1,0:T(8,128)S(1)}, f32[128,64]{1,0:T(8,128)S(1)}, u32[]{:S(2)}, u32[]{:S(2)}) collective-permute-start(f32[128,64]{1,0:T(8,128)S(1)} %maximum_select_fusion.1), channel_id=1, source_target_pairs={{0,16},{2,18},{4,20},{6,22},{8,24},{10,26},{12,28},{14,30},{16,0},... | collective-permute-start | bytes 98312 | tf_op jit(solution)/shard_map/ppermute | solution.py:14
  300.2 62.1 %collective-permute-start.32 = (bf16[2,64,3584]{2,1,0:T(8,128)(2,1)S(1)}, bf16[2,64,3584]{2,1,0:T(8,128)(2,1)S(1)}, u32[]{:S(2)}, u32[]{:S(2)}) collective-permute-start(bf16[2,64,3584]{2,1,0:T(8,128)(2,1)S(1)} %pad_maximum_fusion.13), channel_id=1, source_target_pairs={{0,2},{2,0},{4,6},{6,4},{8,10},{10,8},{12,14},{14,12},{16,18},{18,... | collective-permute-start | bytes 2752520 | tf_op jit(solution)/shard_map/ppermute | solution.py:124
  307.1 55.4 %collective-permute-start.46 = (bf16[2,64,3584]{2,1,0:T(8,128)(2,1)S(1)}, bf16[2,64,3584]{2,1,0:T(8,128)(2,1)}, u32[]{:S(2)}, u32[]{:S(2)}) collective-permute-start(bf16[2,64,3584]{2,1,0:T(8,128)(2,1)S(1)} %pad_maximum_fusion.17), channel_id=1, source_target_pairs={{0,2},{2,0},{4,6},{6,4},{8,10},{10,8},{12,14},{14,12},{16,18},{18,... | collective-permute-start | bytes 2752520 | tf_op jit(solution)/shard_map/ppermute | solution.py:124
  320.9 44.8 %collective-permute-start.50 = (bf16[2,64,3584]{2,1,0:T(8,128)(2,1)S(1)}, bf16[2,64,3584]{2,1,0:T(8,128)(2,1)S(1)}, u32[]{:S(2)}, u32[]{:S(2)}) collective-permute-start(bf16[2,64,3584]{2,1,0:T(8,128)(2,1)S(1)} %pad_maximum_fusion.19), channel_id=1, source_target_pairs={{0,2},{2,0},{4,6},{6,4},{8,10},{10,8},{12,14},{14,12},{16,18},{18,... | collective-permute-start | bytes 2752520 | tf_op jit(solution)/shard_map/ppermute | solution.py:124
  322.1 43.8 %collective-permute-start.42 = (bf16[2,64,3584]{2,1,0:T(8,128)(2,1)S(1)}, bf16[2,64,3584]{2,1,0:T(8,128)(2,1)S(1)}, u32[]{:S(2)}, u32[]{:S(2)}) collective-permute-start(bf16[2,64,3584]{2,1,0:T(8,128)(2,1)S(1)} %pad_maximum_fusion.15), channel_id=1, source_target_pairs={{0,2},{2,0},{4,6},{6,4},{8,10},{10,8},{12,14},{14,12},{16,18},{18,... | collective-permute-start | bytes 2752520 | tf_op jit(solution)/shard_map/ppermute | solution.py:124
  327.6 38.5 %collective-permute-start.4 = (bf16[2,64,3584]{2,1,0:T(8,128)(2,1)S(1)}, bf16[2,64,3584]{2,1,0:T(8,128)(2,1)}, u32[]{:S(2)}, u32[]{:S(2)}) collective-permute-start(bf16[2,64,3584]{2,1,0:T(8,128)(2,1)S(1)} %pad_maximum_fusion.5), channel_id=1, source_target_pairs={{0,4},{2,6},{4,0},{6,2},{8,12},{10,14},{12,8},{14,10},{16,20},{18,... | collective-permute-start | bytes 2752520 | tf_op jit(solution)/shard_map/ppermute | solution.py:124
  362.3 23.3 %collective-permute-start.18 = (bf16[2,64,3584]{2,1,0:T(8,128)(2,1)S(1)}, bf16[2,64,3584]{2,1,0:T(8,128)(2,1)S(1)}, u32[]{:S(2)}, u32[]{:S(2)}) collective-permute-start(bf16[2,64,3584]{2,1,0:T(8,128)(2,1)S(1)} %pad_maximum_fusion.9), channel_id=1, source_target_pairs={{0,4},{2,6},{4,0},{6,2},{8,12},{10,14},{12,8},{14,10},{16,20},{18,... | collective-permute-start | bytes 2752520 | tf_op jit(solution)/shard_map/ppermute | solution.py:124
  362.5 49.8 %collective-permute-start.22 = (bf16[2,64,3584]{2,1,0:T(8,128)(2,1)S(1)}, bf16[2,64,3584]{2,1,0:T(8,128)(2,1)S(1)}, u32[]{:S(2)}, u32[]{:S(2)}) collective-permute-start(bf16[2,64,3584]{2,1,0:T(8,128)(2,1)S(1)} %pad_maximum_fusion.11), channel_id=1, source_target_pairs={{0,4},{2,6},{4,0},{6,2},{8,12},{10,14},{12,8},{14,10},{16,20},{18,... | collective-permute-start | bytes 2752520 | tf_op jit(solution)/shard_map/ppermute | solution.py:124
  365.7 44.4 %collective-permute-start.14 = (bf16[2,64,3584]{2,1,0:T(8,128)(2,1)S(1)}, bf16[2,64,3584]{2,1,0:T(8,128)(2,1)S(1)}, u32[]{:S(2)}, u32[]{:S(2)}) collective-permute-start(bf16[2,64,3584]{2,1,0:T(8,128)(2,1)S(1)} %pad_maximum_fusion.7), channel_id=1, source_target_pairs={{0,4},{2,6},{4,0},{6,2},{8,12},{10,14},{12,8},{14,10},{16,20},{18,... | collective-permute-start | bytes 2752520 | tf_op jit(solution)/shard_map/ppermute | solution.py:124
  365.9 138.5 %collective-permute-start.62 = (bf16[3584,512]{1,0:T(8,128)(2,1)S(1)}, bf16[3584,512]{1,0:T(8,128)(2,1)}, u32[]{:S(2)}, u32[]{:S(2)}) collective-permute-start(bf16[3584,512]{1,0:T(8,128)(2,1)S(1)} %copy-done.43), channel_id=1, source_target_pairs={{0,1},{1,0},{2,3},{3,2},{4,5},{5,4},{6,7},{7,6},{8,9},{9,8},{10,11... | collective-permute-start | bytes 11010056 | tf_op jit(solution)/shard_map/ppermute | solution.py:250
  366.1 145.4 %collective-permute-start.63 = (bf16[512,3584]{1,0:T(8,128)(2,1)}, bf16[512,3584]{1,0:T(8,128)(2,1)S(1)}, u32[]{:S(2)}, u32[]{:S(2)}) collective-permute-start(bf16[512,3584]{1,0:T(8,128)(2,1)} %convolution_convert_fusion), channel_id=1, source_target_pairs={{0,1},{1,0},{2,3},{3,2},{4,5},{5,4},{6,7},{7,6},{8,9},{9,8},{10,11... | collective-permute-start | bytes 11010056 | tf_op jit(solution)/shard_map/ppermute | solution.py:249
  385.6 41.6 %collective-permute-start.51 = (bf16[64,3584]{1,0:T(8,128)(2,1)S(1)}, bf16[64,3584]{1,0:T(8,128)(2,1)S(1)}, u32[]{:S(2)}, u32[]{:S(2)}) collective-permute-start(bf16[64,3584]{1,0:T(8,128)(2,1)S(1)} %fusion.102), channel_id=1, source_target_pairs={{0,4},{2,6},{4,0},{6,2},{8,12},{10,14},{12,8},{14,10},{16,20},{18,... | collective-permute-start | bytes 1376264 | tf_op jit(solution)/shard_map/ppermute | solution.py:124
  410.1 14.5 %collective-permute-start.43 = (bf16[64,3584]{1,0:T(8,128)(2,1)S(1)}, bf16[64,3584]{1,0:T(8,128)(2,1)S(1)}, u32[]{:S(2)}, u32[]{:S(2)}) collective-permute-start(bf16[64,3584]{1,0:T(8,128)(2,1)S(1)} %fusion.106), channel_id=1, source_target_pairs={{0,4},{2,6},{4,0},{6,2},{8,12},{10,14},{12,8},{14,10},{16,20},{18,... | collective-permute-start | bytes 1376264 | tf_op jit(solution)/shard_map/ppermute | solution.py:124
  412.2 14.1 %collective-permute-start.15 = (bf16[64,3584]{1,0:T(8,128)(2,1)S(1)}, bf16[64,3584]{1,0:T(8,128)(2,1)S(1)}, u32[]{:S(2)}, u32[]{:S(2)}) collective-permute-start(bf16[64,3584]{1,0:T(8,128)(2,1)S(1)} %fusion.114), channel_id=1, source_target_pairs={{0,2},{2,0},{4,6},{6,4},{8,10},{10,8},{12,14},{14,12},{16,18},{18,... | collective-permute-start | bytes 1376264 | tf_op jit(solution)/shard_map/ppermute | solution.py:124
  424.8 16.8 %collective-permute-start.55 = (bf16[64,3584]{1,0:T(8,128)(2,1)S(1)}, bf16[64,3584]{1,0:T(8,128)(2,1)S(1)}, u32[]{:S(2)}, u32[]{:S(2)}) collective-permute-start(bf16[64,3584]{1,0:T(8,128)(2,1)S(1)} %add_convert_fusion.7), channel_id=1, source_target_pairs={{24,16},{26,18},{28,20},{30,22},{25,17},{27,19},{29,21},{31,23}} | collective-permute-start | bytes 1376264 | tf_op jit(solution)/shard_map/ppermute | solution.py:128
  426.3 16.5 %collective-permute-start.52 = (bf16[64,3584]{1,0:T(8,128)(2,1)S(1)}, bf16[64,3584]{1,0:T(8,128)(2,1)S(1)}, u32[]{:S(2)}, u32[]{:S(2)}) collective-permute-start(bf16[64,3584]{1,0:T(8,128)(2,1)S(1)} %add_convert_fusion.7), channel_id=1, source_target_pairs={{0,8},{2,10},{4,12},{6,14},{1,9},{3,11},{5,13},{7,15}} | collective-permute-start | bytes 1376264 | tf_op jit(solution)/shard_map/ppermute | solution.py:128
  427.2 16.7 %collective-permute-start.23 = (bf16[64,3584]{1,0:T(8,128)(2,1)S(1)}, bf16[64,3584]{1,0:T(8,128)(2,1)S(1)}, u32[]{:S(2)}, u32[]{:S(2)}) collective-permute-start(bf16[64,3584]{1,0:T(8,128)(2,1)S(1)} %fusion.110), channel_id=1, source_target_pairs={{0,2},{2,0},{4,6},{6,4},{8,10},{10,8},{12,14},{14,12},{16,18},{18,... | collective-permute-start | bytes 1376264 | tf_op jit(solution)/shard_map/ppermute | solution.py:124
  441.6 14.6 %collective-permute-start.27 = (bf16[64,3584]{1,0:T(8,128)(2,1)S(1)}, bf16[64,3584]{1,0:T(8,128)(2,1)S(1)}, u32[]{:S(2)}, u32[]{:S(2)}) collective-permute-start(bf16[64,3584]{1,0:T(8,128)(2,1)S(1)} %add_convert_fusion.14), channel_id=1, source_target_pairs={{24,16},{26,18},{28,20},{30,22},{25,17},{27,19},{29,21},{31,23}} | collective-permute-start | bytes 1376264 | tf_op jit(solution)/shard_map/ppermute | solution.py:128
  442.9 14.6 %collective-permute-start.24 = (bf16[64,3584]{1,0:T(8,128)(2,1)S(1)}, bf16[64,3584]{1,0:T(8,128)(2,1)S(1)}, u32[]{:S(2)}, u32[]{:S(2)}) collective-permute-start(bf16[64,3584]{1,0:T(8,128)(2,1)S(1)} %add_convert_fusion.14), channel_id=1, source_target_pairs={{0,8},{2,10},{4,12},{6,14},{1,9},{3,11},{5,13},{7,15}} | collective-permute-start | bytes 1376264 | tf_op jit(solution)/shard_map/ppermute | solution.py:128
  443.9 18.4 %collective-permute-start.47 = (bf16[64,3584]{1,0:T(8,128)(2,1)S(1)}, bf16[64,3584]{1,0:T(8,128)(2,1)S(1)}, u32[]{:S(2)}, u32[]{:S(2)}) collective-permute-start(bf16[64,3584]{1,0:T(8,128)(2,1)S(1)} %fusion.104), channel_id=1, source_target_pairs={{0,4},{2,6},{4,0},{6,2},{8,12},{10,14},{12,8},{14,10},{16,20},{18,... | collective-permute-start | bytes 1376264 | tf_op jit(solution)/shard_map/ppermute | solution.py:124
  456.2 10.4 %collective-permute-start.53 = (bf16[64,3584]{1,0:T(8,128)(2,1)S(1)}, bf16[64,3584]{1,0:T(8,128)(2,1)S(1)}, u32[]{:S(2)}, u32[]{:S(2)}) collective-permute-start(bf16[64,3584]{1,0:T(8,128)(2,1)S(1)} %get-tuple-element.23), channel_id=1, source_target_pairs={{0,8},{2,10},{4,12},{6,14},{8,16},{10,18},{12,20},{14,22},{1,9},{3... | collective-permute-start | bytes 1376264 | tf_op jit(solution)/shard_map/ppermute | solution.py:128
  457.5 13.5 %collective-permute-start.56 = (bf16[64,3584]{1,0:T(8,128)(2,1)S(1)}, bf16[64,3584]{1,0:T(8,128)(2,1)S(1)}, u32[]{:S(2)}, u32[]{:S(2)}) collective-permute-start(bf16[64,3584]{1,0:T(8,128)(2,1)S(1)} %get-tuple-element.24), channel_id=1, source_target_pairs={{24,16},{26,18},{28,20},{30,22},{16,8},{18,10},{20,12},{22,14},{25... | collective-permute-start | bytes 1376264 | tf_op jit(solution)/shard_map/ppermute | solution.py:128
  462.4 12.2 %collective-permute-start.19 = (bf16[64,3584]{1,0:T(8,128)(2,1)S(1)}, bf16[64,3584]{1,0:T(8,128)(2,1)S(1)}, u32[]{:S(2)}, u32[]{:S(2)}) collective-permute-start(bf16[64,3584]{1,0:T(8,128)(2,1)S(1)} %fusion.112), channel_id=1, source_target_pairs={{0,2},{2,0},{4,6},{6,4},{8,10},{10,8},{12,14},{14,12},{16,18},{18,... | collective-permute-start | bytes 1376264 | tf_op jit(solution)/shard_map/ppermute | solution.py:124
  466.5 10.4 %collective-permute-start.25 = (bf16[64,3584]{1,0:T(8,128)(2,1)S(1)}, bf16[64,3584]{1,0:T(8,128)(2,1)S(1)}, u32[]{:S(2)}, u32[]{:S(2)}) collective-permute-start(bf16[64,3584]{1,0:T(8,128)(2,1)S(1)} %get-tuple-element.25), channel_id=1, source_target_pairs={{0,8},{2,10},{4,12},{6,14},{8,16},{10,18},{12,20},{14,22},{1,9},{3... | collective-permute-start | bytes 1376264 | tf_op jit(solution)/shard_map/ppermute | solution.py:128
  471.0 10.4 %collective-permute-start.28 = (bf16[64,3584]{1,0:T(8,128)(2,1)S(1)}, bf16[64,3584]{1,0:T(8,128)(2,1)S(1)}, u32[]{:S(2)}, u32[]{:S(2)}) collective-permute-start(bf16[64,3584]{1,0:T(8,128)(2,1)S(1)} %get-tuple-element.26), channel_id=1, source_target_pairs={{24,16},{26,18},{28,20},{30,22},{16,8},{18,10},{20,12},{22,14},{25... | collective-permute-start | bytes 1376264 | tf_op jit(solution)/shard_map/ppermute | solution.py:128
  474.6 9.6 %collective-permute-start.33 = (bf16[64,3584]{1,0:T(8,128)(2,1)S(1)}, bf16[64,3584]{1,0:T(8,128)(2,1)S(1)}, u32[]{:S(2)}, u32[]{:S(2)}) collective-permute-start(bf16[64,3584]{1,0:T(8,128)(2,1)S(1)} %fusion.108), channel_id=1, source_target_pairs={{0,4},{2,6},{4,0},{6,2},{8,12},{10,14},{12,8},{14,10},{16,20},{18,... | collective-permute-start | bytes 1376264 | tf_op jit(solution)/shard_map/ppermute | solution.py:124
  476.9 10.4 %collective-permute-start.54 = (bf16[64,3584]{1,0:T(8,128)(2,1)S(1)}, bf16[64,3584]{1,0:T(8,128)(2,1)S(1)}, u32[]{:S(2)}, u32[]{:S(2)}) collective-permute-start(bf16[64,3584]{1,0:T(8,128)(2,1)S(1)} %get-tuple-element.19), channel_id=1, source_target_pairs={{0,8},{2,10},{4,12},{6,14},{8,16},{10,18},{12,20},{14,22},{16,24},... | collective-permute-start | bytes 1376264 | tf_op jit(solution)/shard_map/ppermute | solution.py:128
  481.3 10.6 %collective-permute-start.57 = (bf16[64,3584]{1,0:T(8,128)(2,1)S(1)}, bf16[64,3584]{1,0:T(8,128)(2,1)S(1)}, u32[]{:S(2)}, u32[]{:S(2)}) collective-permute-start(bf16[64,3584]{1,0:T(8,128)(2,1)S(1)} %get-tuple-element.20), channel_id=1, source_target_pairs={{24,16},{26,18},{28,20},{30,22},{16,8},{18,10},{20,12},{22,14},{8,... | collective-permute-start | bytes 1376264 | tf_op jit(solution)/shard_map/ppermute | solution.py:128
  484.2 11.0 %collective-permute-start.5 = (bf16[64,3584]{1,0:T(8,128)(2,1)S(1)}, bf16[64,3584]{1,0:T(8,128)(2,1)S(1)}, u32[]{:S(2)}, u32[]{:S(2)}) collective-permute-start(bf16[64,3584]{1,0:T(8,128)(2,1)S(1)} %fusion.116), channel_id=1, source_target_pairs={{0,2},{2,0},{4,6},{6,4},{8,10},{10,8},{12,14},{14,12},{16,18},{18,... | collective-permute-start | bytes 1376264 | tf_op jit(solution)/shard_map/ppermute | solution.py:124
  487.2 10.4 %collective-permute-start.26 = (bf16[64,3584]{1,0:T(8,128)(2,1)S(1)}, bf16[64,3584]{1,0:T(8,128)(2,1)S(1)}, u32[]{:S(2)}, u32[]{:S(2)}) collective-permute-start(bf16[64,3584]{1,0:T(8,128)(2,1)S(1)} %get-tuple-element.21), channel_id=1, source_target_pairs={{0,8},{2,10},{4,12},{6,14},{8,16},{10,18},{12,20},{14,22},{16,24},... | collective-permute-start | bytes 1376264 | tf_op jit(solution)/shard_map/ppermute | solution.py:128
  492.0 10.4 %collective-permute-start.29 = (bf16[64,3584]{1,0:T(8,128)(2,1)S(1)}, bf16[64,3584]{1,0:T(8,128)(2,1)S(1)}, u32[]{:S(2)}, u32[]{:S(2)}) collective-permute-start(bf16[64,3584]{1,0:T(8,128)(2,1)S(1)} %get-tuple-element.22), channel_id=1, source_target_pairs={{24,16},{26,18},{28,20},{30,22},{16,8},{18,10},{20,12},{22,14},{8,... | collective-permute-start | bytes 1376264 | tf_op jit(solution)/shard_map/ppermute | solution.py:128
  (46 other events, 708.5 us)
